TPU v7x, 256 devices: a whole 4x4x8 slice. The times are simulated.
256 devices in a mesh: pair: 64 (over z, x, y_lo), mo: 4 (over y_hi, core).
Axes of the slice: x: 4, y: 4 (y_hi: 2, y_lo: 2; y = y_hi * 2 + y_lo), z: 8, core: 2. Of those that a mesh axis runs over, the one named last changes fastest.
Arguments:
- integrals: bfloat16 [1024, 1000, 1000], P('pair', 'mo'), may hold values from -6 to 6
- coeffs: bfloat16 [1000, 512], replicated, may hold values from -0.1875 to 0.1875
- mirror: int32 [1024], replicated, may hold values from 0 to 1023, as said below
Outputs:
- combined: float32 [1024, 512, 512], P(None, 'pair', 'mo')
Inputs may be any that keep to these rules, and one draw needn't show every extreme that they name: mirror pairs the rows: mirror[mirror[k]] = k and mirror[k] != k for every row k; a row and its mirror may lie on any devices.
All inputs are finite; a program needn't handle non-finite values.
Results may differ from a plain program's by a relative error of at most 0.0029.
Values may be sent and summed in bfloat16 or wider, within the bound.
A program may use at most 128 MiB of HBM per device.

v0:
```python
import jax
import jax.numpy as jnp
from jax import lax
from jax.sharding import PartitionSpec as P


def on_device(integrals, coeffs, mirror):
    quarter = jnp.einsum(
        "krs,sj->krj", integrals, coeffs, preferred_element_type=jnp.float32
    ).astype(jnp.bfloat16)
    arrived = lax.all_to_all(quarter, "mo", split_axis=2, concat_axis=1, tiled=True)
    half = jnp.einsum("ri,krj->kij", coeffs, arrived, preferred_element_type=jnp.float32)
    pieces = lax.all_to_all(half, "pair", split_axis=1, concat_axis=0, tiled=True)
    partner = jnp.take(pieces, mirror, axis=0)
    return 0.5 * (pieces + partner)


def solution(mesh):
    return jax.shard_map(
        on_device,
        mesh=mesh,
        in_specs=(P("pair", "mo", None), P(), P()),
        out_specs=P(None, "pair", "mo"),
        check_vma=False,
    )
```

profile of v0, /device:TPU:1, one launch (start us, length us, event | category | flops | bytes accessed | tf_op | source)
XLA Modules:
  0.0 237.8 jit_solution(5012048735916774514)
XLA Ops:
  0.0 0.0 copy-start
  0.0 1.2 copy-done
  1.2 23.2 %fusion.4 = bf16[16,250,512]{2,1,0:T(8,128)(2,1)} fusion(bf16[16,250,1000]{2,0,1:T(8,128)(2,1)} %param.3, bf16[1000,512]{1,0:T(8,128)(2,1)S(1)} %copy-done), kind=kOutput, calls=%fused_computation.6 | convolution fusion | flops 4098048000 | bytes 13120000 | tf_op jit(solution)/shard_map/krs,sj->krj/dot_general | solution.py:8
  24.4 7.9 %copy.14 = bf16[16,250,512]{1,0,2:T(8,128)(2,1)} copy(bf16[16,250,512]{2,1,0:T(8,128)(2,1)} %fusion.4) | data formatting | bytes 8192000 | tf_op jit(solution)/shard_map/convert_element_type | solution.py:10
  32.3 57.5 %all_to_all.36 = bf16[16,250,512]{1,0,2:T(8,128)(2,1)} all-to-all(bf16[16,250,512]{1,0,2:T(8,128)(2,1)} %copy.14), channel_id=1, replica_groups=mesh['pair'=64,'mo'=4] {'mo'}, dimensions={2} | all-to-all | bytes 8192000 | tf_op jit(solution)/shard_map/all_to_all | solution.py:11
  89.9 8.5 %copy.16 = bf16[16,4,250,128]{3,0,2,1:T(8,128)(2,1)} copy(bf16[16,4,250,128]{2,0,3,1:T(8,128)(2,1)} %bitcast.18) | data formatting | bytes 8192000 | tf_op jit(solution)/shard_map/all_to_all | solution.py:11
  98.4 6.9 %fusion.7 = f32[16,512,128]{1,2,0:T(8,128)} fusion(bf16[16,1000,128]{2,0,1:T(8,128)(2,1)} %bitcast.17, bf16[1000,512]{1,0:T(8,128)(2,1)S(1)} %copy-done), kind=kOutput, calls=%fused_computation.7 | convolution fusion | flops 2097152000 | bytes 9314304 | tf_op jit(solution)/shard_map/ri,krj->kij/dot_general | solution.py:12
  105.3 5.5 %copy.18 = f32[16,512,128]{2,0,1:T(8,128)} copy(f32[16,512,128]{1,2,0:T(8,128)} %fusion.7) | data formatting | bytes 8388608 | tf_op jit(solution)/shard_map/ri,krj->kij/transpose | solution.py:12
  110.7 0.0 copy-start.1
  110.7 11.3 %all-to-all-start.1 = ((f32[16,512,128]{2,0,1:T(8,128)}), f32[16,512,128]{2,0,1:T(8,128)}, u32[]{:S(2)}, u32[]{:S(2)}) async-start(f32[16,512,128]{2,0,1:T(8,128)} %copy.18), calls=%async_computation.1 | async-start | bytes 8388608 | tf_op jit(solution)/shard_map/all_to_all | solution.py:13
  122.1 0.0 copy-done.1
  122.1 91.3 %all-to-all-done.1 = f32[16,512,128]{2,0,1:T(8,128)} async-done(((f32[16,512,128]{2,0,1:T(8,128)}), f32[16,512,128]{2,0,1:T(8,128)}, u32[]{:S(2)}, u32[]{:S(2)}) %all-to-all-start.1) | async-done | bytes 4194336 | tf_op jit(solution)/shard_map/all_to_all | solution.py:13
  213.4 6.1 %copy.20 = f32[64,16,8,128]{3,2,1,0:T(8,128)} copy(f32[64,16,8,128]{3,1,2,0:T(8,128)} %bitcast.8) | data formatting | bytes 8388608 | tf_op jit(solution)/shard_map/all_to_all | solution.py:13
  219.5 10.2 %gather_fusion = f32[1024,8,128]{2,1,0:T(8,128)} fusion(f32[1024,8,128]{2,1,0:T(8,128)} %bitcast.16, s32[1024]{0:T(1024)S(1)} %fusion.12), kind=kCustom, calls=%fused_computation | custom fusion | bytes 8392704 | tf_op jit(solution)/shard_map/jit(_take)/gather | solution.py:14
  229.7 8.1 %add_multiply_fusion = f32[1024,8,128]{2,1,0:T(8,128)} fusion(f32[1024,8,128]{2,1,0:T(8,128)} %gather_fusion, pred[1024]{0:T(1024)(128)(4,1)S(1)} %compare_and_fusion, f32[64,16,8,128]{3,2,1,0:T(8,128)} %copy.20), kind=kLoop, calls=%fused_computation.3 | loop fusion | flops 3145728 | bytes 12583936 | tf_op jit(solution)/shard_map/mul | solution.py:15
  (2 shorter events, 0.0 us)
Async XLA Ops:
  0.0 1.2 copy-start
  110.7 11.3 %copy-start.1 = (s32[1024]{0:T(1024)S(1)}, s32[1024]{0:T(1024)}, u32[]{:S(2)}) copy-start(s32[1024]{0:T(1024)} %param.5) | copy-start | bytes 12292
  110.7 102.6 %all-to-all-start.1 = ((f32[16,512,128]{2,0,1:T(8,128)}), f32[16,512,128]{2,0,1:T(8,128)}, u32[]{:S(2)}, u32[]{:S(2)}) async-start(f32[16,512,128]{2,0,1:T(8,128)} %copy.18), calls=%async_computation.1 | async-start | bytes 8388608 | tf_op jit(solution)/shard_map/all_to_all | solution.py:13
where the time goes:
time: 242 us; the launch traced here: 238 us
  waiting for transfers between devices  91.3 us (38%)
  blocking collectives  57.5 us (24%)
  local copies, waits for them, and re-layouts  39.5 us (16%)
  matrix products  30.1 us (12%)
  starting transfers between devices  11.3 us (5%)
  other arithmetic  8.1 us (3%)
    all_to_all x1, waiting for transfers between devices, on_device(): lax.all_to_all(half, 'pair', split_axis=1, concat_axis=0, tiled=True)  91.3 us
    all_to_all x1, blocking collectives, on_device(): lax.all_to_all(quarter, 'mo', split_axis=2, concat_axis=1, tiled=True)  57.5 us
    dot_general x1, matrix products, on_device(): jnp.einsum('krs,sj->krj', integrals, coeffs, preferred_element_type=jnp.f...  23.2 us
    all_to_all x1, starting transfers between devices, on_device(): lax.all_to_all(half, 'pair', split_axis=1, concat_axis=0, tiled=True)  11.3 us
    gather x1, local copies, waits for them, and re-layouts, on_device(): partner = jnp.take(pieces, mirror, axis=0)  10.2 us
    all_to_all x1, local copies, waits for them, and re-layouts, on_device(): lax.all_to_all(quarter, 'mo', split_axis=2, concat_axis=1, tiled=True)  8.54 us
    mul x1, other arithmetic, on_device(): return 0.5 * (pieces + partner)  8.09 us
    convert_element_type x1, local copies, waits for them, and re-layouts, on_device(): quarter = jnp.einsum('krs,sj->krj', integrals, coeffs, preferred_element_...  7.91 us
  transfers between devices with their start and end apart: 1, of which 1 were waited for; matrix products, arithmetic and copies ran while one was open for 0% of the time, Pallas kernels for 0%

commit v1 on v0

v1 whole, which is shorter than its diff:
```python
import jax
import jax.numpy as jnp
from jax import lax
from jax.sharding import PartitionSpec as P


def make_on_device(n_pair, n_mo):
    def on_device(integrals, coeffs, mirror):
        rows, r_loc, nbf = integrals.shape
        nmo = coeffs.shape[1]
        c_j = coeffs.reshape(nbf, n_mo, nmo // n_mo).transpose(1, 0, 2)
        quarter = jnp.einsum(
            "krs,bsj->bkrj", integrals, c_j, preferred_element_type=jnp.float32
        ).astype(jnp.bfloat16)
        arrived = lax.all_to_all(quarter, "mo", 0, 0, tiled=True)
        c_r = coeffs.reshape(n_mo, r_loc, n_pair, nmo // n_pair)
        half = jnp.einsum(
            "brpi,bkrj->pkij", c_r, arrived, preferred_element_type=jnp.float32
        )
        pieces = lax.all_to_all(half.astype(jnp.bfloat16), "pair", 0, 0, tiled=True)
        pieces = pieces.reshape(n_pair * rows, nmo // n_pair, nmo // n_mo)
        pieces = pieces.astype(jnp.float32)
        partner = jnp.take(pieces, mirror, axis=0)
        return 0.5 * (pieces + partner)

    return on_device


def solution(mesh):
    return jax.shard_map(
        make_on_device(mesh.shape["pair"], mesh.shape["mo"]),
        mesh=mesh,
        in_specs=(P("pair", "mo", None), P(), P()),
        out_specs=P(None, "pair", "mo"),
        check_vma=False,
    )
```

time: 242 us -> 164 us (0.68)
  blocking collectives: 57.5 us -> 0 us
  local copies, waits for them, and re-layouts: 39.5 us -> 22.1 us
  matrix products: 30.1 us -> 16.9 us
  starting transfers between devices: 11.3 us -> 19.1 us
  waiting for transfers between devices: 91.3 us -> 94 us
    all_to_all x1 -> x0, blocking collectives: 57.5 us -> none  [on_device(): lax.all_to_all(quarter, 'mo', split_axis=2, concat_axis=1, tiled=True)]
    all_to_all x2 -> x0, local copies, waits for them, and re-layouts: 14.7 us -> none  [the longest x1 8.54 us: on_device(): lax.all_to_all(quarter, 'mo', split_axis=2, concat_axis=1, tiled=True)]
    dot_general x2, matrix products: 30.1 us -> 16.9 us  [the longest x1 11.4 us: on_device(): jnp.einsum('krs,bsj->bkrj', integrals, c_j, preferred_element_type=jnp.fl...]
    all_to_all x1 -> x2, starting transfers between devices: 11.3 us -> 19.1 us  [the longest x1 10.9 us: on_device(): pieces = lax.all_to_all(half.astype(jnp.bfloat16), 'pair', 0, 0, tiled=True)]
    transpose x1 -> x0, local copies, waits for them, and re-layouts: 5.46 us -> none  [on_device(): jnp.einsum('ri,krj->kij', coeffs, arrived, preferred_element_type=jnp.flo...]
    all_to_all x1 -> x2, waiting for transfers between devices: 91.3 us -> 94 us  [the longest x1 47.8 us: on_device(): pieces = lax.all_to_all(half.astype(jnp.bfloat16), 'pair', 0, 0, tiled=True)]
    convert_element_type x1 -> x2, local copies, waits for them, and re-layouts: 7.91 us -> 10.2 us  [the longest x1 7.56 us: on_device(): quarter = jnp.einsum('krs,bsj->bkrj', integrals, c_j, preferred_element_t...]
  transfers between devices with their start and end apart: 1 -> 2, of which waited for: 1 -> 2; matrix products, arithmetic and copies ran while one was open for 0% -> 1% of each run, Pallas kernels for 0% -> 0%
where the time goes in v1:
time: 164 us; the launch traced here: 162 us
  waiting for transfers between devices  94 us (57%)
  local copies, waits for them, and re-layouts  22.1 us (13%)
  starting transfers between devices  19.1 us (12%)
  matrix products  16.9 us (10%)
  other arithmetic  9.6 us (6%)
    all_to_all x1, waiting for transfers between devices, on_device(): pieces = lax.all_to_all(half.astype(jnp.bfloat16), 'pair', 0, 0, tiled=True)  47.8 us
    all_to_all x1, waiting for transfers between devices, on_device(): arrived = lax.all_to_all(quarter, 'mo', 0, 0, tiled=True)  46.2 us
    dot_general x1, matrix products, on_device(): jnp.einsum('krs,bsj->bkrj', integrals, c_j, preferred_element_type=jnp.fl...  11.4 us
    all_to_all x1, starting transfers between devices, on_device(): pieces = lax.all_to_all(half.astype(jnp.bfloat16), 'pair', 0, 0, tiled=True)  10.9 us
    gather x1, local copies, waits for them, and re-layouts, on_device(): partner = jnp.take(pieces, mirror, axis=0)  10.3 us
    all_to_all x1, starting transfers between devices, on_device(): arrived = lax.all_to_all(quarter, 'mo', 0, 0, tiled=True)  8.14 us
    convert_element_type x1, local copies, waits for them, and re-layouts, on_device(): quarter = jnp.einsum('krs,bsj->bkrj', integrals, c_j, preferred_element_t...  7.56 us
    mul x1, other arithmetic, on_device(): return 0.5 * (pieces + partner)  7.16 us
  transfers between devices with their start and end apart: 2, of which 2 were waited for; matrix products, arithmetic and copies ran while one was open for 1% of the time, Pallas kernels for 0%

profile of v1, /device:TPU:1, one launch (start us, length us, event | category | flops | bytes accessed | tf_op | source)
XLA Modules:
  0.0 161.7 jit_solution(12293740479334899032)
XLA Ops:
  0.0 11.4 %convert_bitcast_fusion = bf16[4,16,250,128]{2,3,0,1:T(8,128)(2,1)} fusion(bf16[16,250,1000,1]{2,0,1,3:T(8,128)(2,1)} %bitcast.33, bf16[1000,512]{1,0:T(8,128)(2,1)} %param.4), kind=kOutput, calls=%fused_computation.7 | convolution fusion | flops 4098048000 | bytes 13120000 | tf_op jit(solution)/shard_map/krs,bsj->bkrj/dot_general | solution.py:12
  11.4 7.6 %copy.10 = bf16[4,16,250,128]{3,1,2,0:T(8,128)(2,1)} copy(bf16[4,16,250,128]{2,3,0,1:T(8,128)(2,1)} %convert_bitcast_fusion) | data formatting | bytes 8192000 | tf_op jit(solution)/shard_map/convert_element_type | solution.py:14
  18.9 0.0 copy-start
  18.9 8.1 %all-to-all-start = ((bf16[4,16,250,128]{3,1,2,0:T(8,128)(2,1)}), bf16[4,16,250,128]{3,1,2,0:T(8,128)(2,1)}, u32[]{:S(2)}, u32[]{:S(2)}) async-start(bf16[4,16,250,128]{3,1,2,0:T(8,128)(2,1)} %copy.10), calls=%async_computation | async-start | bytes 8192000 | tf_op jit(solution)/shard_map/all_to_all | solution.py:15
  27.1 0.0 copy-done
  27.1 0.5 copy.11
  27.6 1.1 reshape.15
  28.7 46.2 %all-to-all-done = bf16[4,16,250,128]{3,1,2,0:T(8,128)(2,1)} async-done(((bf16[4,16,250,128]{3,1,2,0:T(8,128)(2,1)}), bf16[4,16,250,128]{3,1,2,0:T(8,128)(2,1)}, u32[]{:S(2)}, u32[]{:S(2)}) %all-to-all-start) | async-done | bytes 4096032 | tf_op jit(solution)/shard_map/all_to_all | solution.py:15
  74.9 5.5 %fusion.6 = bf16[64,16,8,128]{3,0,2,1:T(8,128)(2,1)S(1)} fusion(bf16[4,16,250,128,1]{3,1,2,0,4:T(8,128)(2,1)} %bitcast.4, bf16[4,250,64,8]{1,0,3,2:T(4,128)(2,1)S(1)} %reshape.15), kind=kOutput, calls=%fused_computation.8 | convolution fusion | flops 2098200576 | bytes 7217152 | tf_op jit(solution)/shard_map/brpi,bkrj->pkij/dot_general | solution.py:17
  80.5 0.0 copy-start.1
  80.5 2.7 %copy.14 = bf16[64,16,8,128]{3,2,1,0:T(8,128)(2,1)} copy(bf16[64,16,8,128]{3,0,2,1:T(8,128)(2,1)S(1)} %fusion.6) | data formatting | bytes 4194304 | tf_op jit(solution)/shard_map/convert_element_type | solution.py:20
  83.2 10.9 %all-to-all-start.1 = ((bf16[64,16,8,128]{3,2,1,0:T(8,128)(2,1)}), bf16[64,16,8,128]{3,2,1,0:T(8,128)(2,1)S(1)}, u32[]{:S(2)}, u32[]{:S(2)}) async-start(bf16[64,16,8,128]{3,2,1,0:T(8,128)(2,1)} %copy.14), calls=%async_computation.1 | async-start | bytes 4194304 | tf_op jit(solution)/shard_map/all_to_all | solution.py:20
  94.1 0.0 copy-done.1
  94.1 47.8 %all-to-all-done.1 = bf16[64,16,8,128]{3,2,1,0:T(8,128)(2,1)S(1)} async-done(((bf16[64,16,8,128]{3,2,1,0:T(8,128)(2,1)}), bf16[64,16,8,128]{3,2,1,0:T(8,128)(2,1)S(1)}, u32[]{:S(2)}, u32[]{:S(2)}) %all-to-all-start.1) | async-done | bytes 2097184 | tf_op jit(solution)/shard_map/all_to_all | solution.py:20
  141.9 2.4 %bitcast_convert_fusion.1 = f32[1024,8,128]{2,1,0:T(8,128)} fusion(bf16[64,16,8,128]{3,2,1,0:T(8,128)(2,1)S(1)} %all-to-all-done.1), kind=kLoop, calls=%fused_computation.9 | loop fusion | flops 1048576 | bytes 6291456 | tf_op jit(solution)/shard_map/convert_element_type | solution.py:22
  144.3 10.3 %gather_fusion = f32[1024,8,128]{2,1,0:T(8,128)} fusion(f32[1024,8,128]{2,1,0:T(8,128)} %bitcast_convert_fusion.1, s32[1024]{0:T(1024)S(1)} %fusion.12), kind=kCustom, calls=%fused_computation | custom fusion | bytes 8392704 | tf_op jit(solution)/shard_map/jit(_take)/gather | solution.py:23
  154.6 7.2 %add_multiply_fusion = f32[1024,8,128]{2,1,0:T(8,128)} fusion(f32[1024,8,128]{2,1,0:T(8,128)} %gather_fusion, pred[1024]{0:T(1024)(128)(4,1)S(1)} %compare_and_fusion, bf16[64,16,8,128]{3,2,1,0:T(8,128)(2,1)S(1)} %all-to-all-done.1), kind=kLoop, calls=%fused_computation.6 | loop fusion | flops 4194304 | bytes 10486784 | tf_op jit(solution)/shard_map/mul | solution.py:24
  (2 shorter events, 0.0 us)
Async XLA Ops:
  18.9 8.1 %copy-start = (bf16[1000,512]{1,0:T(8,128)(2,1)S(1)}, bf16[1000,512]{1,0:T(8,128)(2,1)}, u32[]{:S(2)}) copy-start(bf16[1000,512]{1,0:T(8,128)(2,1)} %param.4) | copy-start | bytes 3072004
  18.9 56.0 %all-to-all-start = ((bf16[4,16,250,128]{3,1,2,0:T(8,128)(2,1)}), bf16[4,16,250,128]{3,1,2,0:T(8,128)(2,1)}, u32[]{:S(2)}, u32[]{:S(2)}) async-start(bf16[4,16,250,128]{3,1,2,0:T(8,128)(2,1)} %copy.10), calls=%async_computation | async-start | bytes 8192000 | tf_op jit(solution)/shard_map/all_to_all | solution.py:15
  80.5 13.6 %copy-start.1 = (s32[1024]{0:T(1024)S(1)}, s32[1024]{0:T(1024)}, u32[]{:S(2)}) copy-start(s32[1024]{0:T(1024)} %param.5) | copy-start | bytes 12292
  83.2 58.7 %all-to-all-start.1 = ((bf16[64,16,8,128]{3,2,1,0:T(8,128)(2,1)}), bf16[64,16,8,128]{3,2,1,0:T(8,128)(2,1)S(1)}, u32[]{:S(2)}, u32[]{:S(2)}) async-start(bf16[64,16,8,128]{3,2,1,0:T(8,128)(2,1)} %copy.14), calls=%async_computation.1 | async-start | bytes 4194304 | tf_op jit(solution)/shard_map/all_to_all | solution.py:20

commit v2 on v1

--- a/solution.py
+++ b/solution.py
@@ -1,7 +1,31 @@
 import jax
 import jax.numpy as jnp
 from jax import lax
+from jax.experimental import pallas as pl
+from jax.experimental.pallas import tpu as pltpu
 from jax.sharding import PartitionSpec as P
+
+
+def combine_kernel(mirror_ref, x_ref, o_ref):
+    def body(k, carry):
+        a = x_ref[k].astype(jnp.float32)
+        b = x_ref[mirror_ref[k]].astype(jnp.float32)
+        o_ref[k] = 0.5 * (a + b)
+        return carry
+
+    lax.fori_loop(0, x_ref.shape[0], body, 0, unroll=8)
+
+
+def combine(pieces, mirror):
+    return pl.pallas_call(
+        combine_kernel,
+        out_shape=jax.ShapeDtypeStruct(pieces.shape, jnp.float32),
+        in_specs=[
+            pl.BlockSpec(memory_space=pltpu.SMEM),
+            pl.BlockSpec(memory_space=pltpu.VMEM),
+        ],
+        out_specs=pl.BlockSpec(memory_space=pltpu.VMEM),
+    )(mirror, pieces)
 
 
 def make_on_device(n_pair, n_mo):
@@ -19,9 +43,7 @@
         )
         pieces = lax.all_to_all(half.astype(jnp.bfloat16), "pair", 0, 0, tiled=True)
         pieces = pieces.reshape(n_pair * rows, nmo // n_pair, nmo // n_mo)
-        pieces = pieces.astype(jnp.float32)
-        partner = jnp.take(pieces, mirror, axis=0)
-        return 0.5 * (pieces + partner)
+        return combine(pieces, mirror)
 
     return on_device
 

time: 164 us -> 149 us (0.909)
  blocking collectives: 0 us -> 58.6 us
  waiting for transfers between devices: 94 us -> 46.2 us
  local copies, waits for them, and re-layouts: 22.1 us -> 10.5 us
  starting transfers between devices: 19.1 us -> 8.16 us
  other arithmetic: 9.6 us -> 0 us
  Pallas kernels: 0 us -> 5.7 us
    all_to_all x0 -> x1, blocking collectives: none -> 58.6 us  [on_device(): pieces = lax.all_to_all(half.astype(jnp.bfloat16), 'pair', 0, 0, tiled=True)]
    all_to_all x1 -> x0, waiting for transfers between devices: 47.8 us -> none  [on_device(): pieces = lax.all_to_all(half.astype(jnp.bfloat16), 'pair', 0, 0, tiled=True)]
    all_to_all x1 -> x0, starting transfers between devices: 10.9 us -> none  [on_device(): pieces = lax.all_to_all(half.astype(jnp.bfloat16), 'pair', 0, 0, tiled=True)]
    gather x1 -> x0, local copies, waits for them, and re-layouts: 10.3 us -> none  [on_device(): partner = jnp.take(pieces, mirror, axis=0)]
    mul x1 -> x0, other arithmetic: 7.16 us -> none  [on_device(): return 0.5 * (pieces + partner)]
    pallas_call x0 -> x1, Pallas kernels: none -> 5.7 us  [combine(): pl.pallas_call(combine_kernel, out_shape=jax.ShapeDtypeStruct(pieces.shap...]
    convert_element_type x1 -> x0, other arithmetic: 2.42 us -> none  [on_device(): pieces = pieces.astype(jnp.float32)]
  transfers between devices with their start and end apart: 2 -> 1, of which waited for: 2 -> 1; matrix products, arithmetic and copies ran while one was open for 1% -> 1% of each run, Pallas kernels for 0% -> 0%
where the time goes in v2:
time: 149 us; the launch traced here: 146 us
  blocking collectives  58.6 us (39%)
  waiting for transfers between devices  46.2 us (31%)
  matrix products  16.9 us (11%)
  local copies, waits for them, and re-layouts  10.5 us (7%)
  starting transfers between devices  8.16 us (5%)
  Pallas kernels  5.7 us (4%)
    all_to_all x1, blocking collectives, on_device(): pieces = lax.all_to_all(half.astype(jnp.bfloat16), 'pair', 0, 0, tiled=True)  58.6 us
    all_to_all x1, waiting for transfers between devices, on_device(): arrived = lax.all_to_all(quarter, 'mo', 0, 0, tiled=True)  46.2 us
    dot_general x1, matrix products, on_device(): jnp.einsum('krs,bsj->bkrj', integrals, c_j, preferred_element_type=jnp.fl...  11.4 us
    all_to_all x1, starting transfers between devices, on_device(): arrived = lax.all_to_all(quarter, 'mo', 0, 0, tiled=True)  8.16 us
    convert_element_type x1, local copies, waits for them, and re-layouts, on_device(): quarter = jnp.einsum('krs,bsj->bkrj', integrals, c_j, preferred_element_t...  7.55 us
    pallas_call x1, Pallas kernels, combine(): pl.pallas_call(combine_kernel, out_shape=jax.ShapeDtypeStruct(pieces.shap...  5.7 us
    dot_general x1, matrix products, on_device(): jnp.einsum('brpi,bkrj->pkij', c_r, arrived, preferred_element_type=jnp.fl...  5.54 us
  transfers between devices with their start and end apart: 1, of which 1 were waited for; matrix products, arithmetic and copies ran while one was open for 1% of the time, Pallas kernels for 0%

profile of v2, /device:TPU:1, one launch (start us, length us, event | category | flops | bytes accessed | tf_op | source)
XLA Modules:
  0.0 146.2 jit_solution(14646365101517208778)
XLA Ops:
  0.0 11.4 %convert_bitcast_fusion = bf16[4,16,250,128]{2,3,0,1:T(8,128)(2,1)} fusion(bf16[16,250,1000,1]{2,0,1,3:T(8,128)(2,1)} %bitcast.30, bf16[1000,512]{1,0:T(8,128)(2,1)} %param.4), kind=kOutput, calls=%fused_computation.5 | convolution fusion | flops 4098048000 | bytes 13120000 | tf_op jit(solution)/shard_map/krs,bsj->bkrj/dot_general | solution.py:36
  11.4 7.6 %copy.11 = bf16[4,16,250,128]{3,1,2,0:T(8,128)(2,1)} copy(bf16[4,16,250,128]{2,3,0,1:T(8,128)(2,1)} %convert_bitcast_fusion) | data formatting | bytes 8192000 | tf_op jit(solution)/shard_map/convert_element_type | solution.py:38
  18.9 0.0 copy-start
  18.9 8.2 %all-to-all-start = ((bf16[4,16,250,128]{3,1,2,0:T(8,128)(2,1)}), bf16[4,16,250,128]{3,1,2,0:T(8,128)(2,1)}, u32[]{:S(2)}, u32[]{:S(2)}) async-start(bf16[4,16,250,128]{3,1,2,0:T(8,128)(2,1)} %copy.11), calls=%async_computation | async-start | bytes 8192000 | tf_op jit(solution)/shard_map/all_to_all | solution.py:39
  27.1 0.0 copy-done
  27.1 0.5 copy.12
  27.6 1.1 reshape.10
  28.7 46.2 %all-to-all-done = bf16[4,16,250,128]{3,1,2,0:T(8,128)(2,1)} async-done(((bf16[4,16,250,128]{3,1,2,0:T(8,128)(2,1)}), bf16[4,16,250,128]{3,1,2,0:T(8,128)(2,1)}, u32[]{:S(2)}, u32[]{:S(2)}) %all-to-all-start) | async-done | bytes 4096032 | tf_op jit(solution)/shard_map/all_to_all | solution.py:39
  74.9 5.5 %fusion.6 = bf16[64,16,8,128]{3,0,2,1:T(8,128)(2,1)S(1)} fusion(bf16[4,16,250,128,1]{3,1,2,0,4:T(8,128)(2,1)} %bitcast.4, bf16[4,250,64,8]{1,0,3,2:T(4,128)(2,1)S(1)} %reshape.10), kind=kOutput, calls=%fused_computation.6 | convolution fusion | flops 2098200576 | bytes 7217152 | tf_op jit(solution)/shard_map/brpi,bkrj->pkij/dot_general | solution.py:41
  80.5 1.4 copy.15
  81.8 58.6 %all_to_all.10 = bf16[64,16,8,128]{3,2,1,0:T(8,128)(2,1)} all-to-all(bf16[64,16,8,128]{3,2,1,0:T(8,128)(2,1)S(1)} %copy.15), channel_id=1, replica_groups=mesh['pair'=64,'mo'=4] {'pair'}, dimensions={0} | all-to-all | bytes 4194304 | tf_op jit(solution)/shard_map/all_to_all | solution.py:44
  140.5 5.7 %shard_map.37 = f32[1024,8,128]{2,1,0:T(8,128)} custom-call(s32[1024]{0:T(1024)} %mirror_ref.1, bf16[1024,8,128]{2,1,0:T(8,128)(2,1)} %bitcast.29), custom_call_target="tpu_custom_call" | custom-call | tf_op jit(solution)/shard_map/pallas_call | solution.py:20
Async XLA Ops:
  18.9 8.2 %copy-start = (bf16[1000,512]{1,0:T(8,128)(2,1)S(1)}, bf16[1000,512]{1,0:T(8,128)(2,1)}, u32[]{:S(2)}) copy-start(bf16[1000,512]{1,0:T(8,128)(2,1)} %param.4) | copy-start | bytes 3072004
  18.9 56.0 %all-to-all-start = ((bf16[4,16,250,128]{3,1,2,0:T(8,128)(2,1)}), bf16[4,16,250,128]{3,1,2,0:T(8,128)(2,1)}, u32[]{:S(2)}, u32[]{:S(2)}) async-start(bf16[4,16,250,128]{3,1,2,0:T(8,128)(2,1)} %copy.11), calls=%async_computation | async-start | bytes 8192000 | tf_op jit(solution)/shard_map/all_to_all | solution.py:39

commit v3 on v1

v3 whole, which is shorter than its diff:
```python
import jax
import jax.numpy as jnp
from jax import lax
from jax.experimental import pallas as pl
from jax.experimental.pallas import tpu as pltpu
from jax.sharding import PartitionSpec as P

N_CHUNK = 4


def combine_kernel(mirror_ref, *refs):
    xs, o_ref = refs[:-1], refs[-1]
    n_src, kc = xs[0].shape[0], xs[0].shape[1]
    rows = kc * len(xs)

    def body(src, carry):
        for c, x in enumerate(xs):
            for kk in range(kc):
                k = src * rows + c * kc + kk
                m = mirror_ref[k]
                ms, mc, mk = m // rows, (m % rows) // kc, m % kc
                b = xs[0][ms, mk]
                for c2 in range(1, len(xs)):
                    b = jnp.where(mc == c2, xs[c2][ms, mk], b)
                a = x[src, kk].astype(jnp.float32)
                o_ref[k] = 0.5 * (a + b.astype(jnp.float32))
        return carry

    lax.fori_loop(0, n_src, body, 0)


def combine(chunks, mirror):
    n_src, kc, a, b = chunks[0].shape
    return pl.pallas_call(
        combine_kernel,
        out_shape=jax.ShapeDtypeStruct((n_src * kc * len(chunks), a, b), jnp.float32),
        in_specs=[pl.BlockSpec(memory_space=pltpu.SMEM)]
        + [pl.BlockSpec(memory_space=pltpu.VMEM)] * len(chunks),
        out_specs=pl.BlockSpec(memory_space=pltpu.VMEM),
    )(mirror, *chunks)


def make_on_device(n_pair, n_mo):
    def on_device(integrals, coeffs, mirror):
        rows, r_loc, nbf = integrals.shape
        nmo = coeffs.shape[1]
        kc = rows // N_CHUNK
        c_j = coeffs.reshape(nbf, n_mo, nmo // n_mo).transpose(1, 0, 2)
        c_r = coeffs.reshape(n_mo, r_loc, n_pair, nmo // n_pair)
        outs = []
        me = lax.axis_index("mo")
        for c in range(N_CHUNK):
            block = integrals[c * kc:(c + 1) * kc]
            quarter = jnp.einsum(
                "krs,bsj->bkrj", block, c_j, preferred_element_type=jnp.float32
            ).astype(jnp.bfloat16)
            half = None
            for s in range(n_mo):
                dst = lax.rem(me + s, n_mo)
                src = lax.rem(me + n_mo - s, n_mo)
                piece = lax.dynamic_index_in_dim(quarter, dst, 0, keepdims=False)
                if s:
                    perm = [(i, (i + s) % n_mo) for i in range(n_mo)]
                    piece = lax.ppermute(piece, "mo", perm)
                coef = lax.dynamic_index_in_dim(c_r, src, 0, keepdims=False)
                term = jnp.einsum(
                    "rpi,krj->pkij", coef, piece, preferred_element_type=jnp.float32
                )
                half = term if half is None else half + term
            outs.append(lax.all_to_all(half.astype(jnp.bfloat16), "pair", 0, 0, tiled=True))
        return combine(outs, mirror)

    return on_device


def solution(mesh):
    return jax.shard_map(
        make_on_device(mesh.shape["pair"], mesh.shape["mo"]),
        mesh=mesh,
        in_specs=(P("pair", "mo", None), P(), P()),
        out_specs=P(None, "pair", "mo"),
        check_vma=False,
    )
```

time: 164 us -> 181 us (1.10)
  the two profiles are of different devices: /device:TPU:1 before, /device:TPU:16 now
where the time goes in v3:
time: 181 us; the launch traced here: 180 us
  starting transfers between devices  40.1 us (22%)
  local copies, waits for them, and re-layouts  34.9 us (19%)
  matrix products  32.9 us (18%)
  waiting for transfers between devices  29.9 us (17%)
  blocking collectives  21.7 us (12%)
  Pallas kernels  20 us (11%)
    all_to_all x3, waiting for transfers between devices, on_device(): lax.all_to_all(half.astype(jnp.bfloat16), 'pair', 0, 0, tiled=True)  29.9 us
    all_to_all x3, starting transfers between devices, on_device(): lax.all_to_all(half.astype(jnp.bfloat16), 'pair', 0, 0, tiled=True)  23.6 us
    all_to_all x1, blocking collectives, on_device(): lax.all_to_all(half.astype(jnp.bfloat16), 'pair', 0, 0, tiled=True)  21.7 us
    dot_general x16, matrix products, on_device(): jnp.einsum('rpi,krj->pkij', coef, piece, preferred_element_type=jnp.float32)  21.1 us
    pallas_call x1, Pallas kernels, combine(): pl.pallas_call(combine_kernel, out_shape=jax.ShapeDtypeStruct((n_src * kc...  20 us
    ppermute x12, starting transfers between devices, on_device(): piece = lax.ppermute(piece, 'mo', perm)  16.4 us
    unnamed x29, local copies, waits for them, and re-layouts  16.2 us
    dot_general x4, matrix products, on_device(): jnp.einsum('krs,bsj->bkrj', block, c_j, preferred_element_type=jnp.float32)  11.8 us
  transfers between devices with their start and end apart: 15, of which 3 were waited for; matrix products, arithmetic and copies ran while one was open for 26% of the time, Pallas kernels for 0%

profile of v3, /device:TPU:16, one launch (start us, length us, event | category | flops | bytes accessed | tf_op | source)
XLA Modules:
  0.0 179.8 jit_solution(16992845949967647995)
XLA Ops:
  0.0 9.5 %fusion.84 = (bf16[4,250,1000]{2,0,1:T(4,128)(2,1)}, bf16[4,250,1000]{2,0,1:T(4,128)(2,1)S(1)}, bf16[4,250,1000]{2,0,1:T(4,128)(2,1)}, bf16[4,250,1000]{2,0,1:T(4,128)(2,1)}) fusion(bf16[16,250,1000]{2,0,1:T(8,128)(2,1)} %param.3), kind=kLoop, calls=%fused_computation.101 | loop fusion | bytes 16000000 | tf_op jit(solution)/shard_map/slice | solution.py:53
  9.5 4.4 %copy.147 = bf16[4,250,1000]{1,2,0:T(8,128)(2,1)} copy(bf16[4,250,1000]{2,0,1:T(4,128)(2,1)} %get-tuple-element.5) | data formatting | bytes 4000000
  13.9 2.9 %fusion.17 = bf16[4,128,4,250]{3,1,2,0:T(8,128)(2,1)S(1)} fusion(bf16[4,250,1000]{1,2,0:T(8,128)(2,1)} %copy.147, bf16[1000,512]{1,0:T(8,128)(2,1)S(1)} %copy-done), kind=kOutput, calls=%fused_computation.11 | convolution fusion | flops 1024512000 | bytes 4048000 | tf_op jit(solution)/shard_map/krs,bsj->bkrj/dot_general | solution.py:54
  16.8 1.0 copy-done.8
  17.7 1.0 dynamic-slice_bitcast_fusion.1
  18.7 2.1 %collective-permute-start.10 = (bf16[4,250,128]{1,2,0:T(8,128)(2,1)}, bf16[4,250,128]{1,2,0:T(8,128)(2,1)}, u32[]{:S(2)}, u32[]{:S(2)}) collective-permute-start(bf16[4,250,128]{1,2,0:T(8,128)(2,1)} %get-tuple-element.9), channel_id=1, source_target_pairs={{0,2},{1,3},{2,0},{3,1},{4,6},{5,7},{6,4},{7,5},{8,10},{9,11},{10,... | collective-permute-start | bytes 768008 | tf_op jit(solution)/shard_map/ppermute | solution.py:64
  21.4 2.8 %copy.146 = bf16[4,250,1000]{1,2,0:T(8,128)(2,1)} copy(bf16[4,250,1000]{2,0,1:T(4,128)(2,1)S(1)} %get-tuple-element.6) | data formatting | bytes 4000000
  24.1 2.9 %fusion.14 = bf16[4,128,4,250]{3,1,2,0:T(8,128)(2,1)S(1)} fusion(bf16[4,250,1000]{1,2,0:T(8,128)(2,1)} %copy.146, bf16[1000,512]{1,0:T(8,128)(2,1)S(1)} %copy-done), kind=kOutput, calls=%fused_computation.10 | convolution fusion | flops 1024512000 | bytes 4048000 | tf_op jit(solution)/shard_map/krs,bsj->bkrj/dot_general | solution.py:54
  27.1 1.0 copy-done.6
  28.1 0.9 dynamic-slice_bitcast_fusion.4
  29.0 1.3 collective-permute-start.7
  30.3 2.5 %collective-permute-start.8 = (bf16[4,250,128]{1,2,0:T(8,128)(2,1)}, bf16[4,250,128]{1,2,0:T(8,128)(2,1)}, u32[]{:S(2)}, u32[]{:S(2)}) collective-permute-start(bf16[4,250,128]{1,2,0:T(8,128)(2,1)} %get-tuple-element.13), channel_id=1, source_target_pairs={{0,3},{1,0},{2,1},{3,2},{4,7},{5,4},{6,5},{7,6},{8,11},{9,8},{10,9... | collective-permute-start | bytes 768008 | tf_op jit(solution)/shard_map/ppermute | solution.py:64
  33.3 1.1 reshape.7
  34.4 2.2 %constant_dynamic-slice_fusion.1 = (bf16[1,250,64,8]{1,0,3,2:T(2,128)(2,1)S(1)}, bf16[1,250,64,8]{1,0,3,2:T(2,128)(2,1)S(1)}, bf16[1,250,64,8]{1,0,3,2:T(2,128)(2,1)S(1)}, bf16[1,250,64,8]{1,0,3,2:T(2,128)(2,1)S(1)}) fusion(bf16[4,250,64,8]{1,0,3,2:T(4,128)(2,1)S(1)} %reshape.7, s32[]{:T(128)S(6)} %select_n.48, s32[]{:T(128)S(6)} %select_n.46, ...), kind=kLoop, calls=%fused_computation.97 | loop fusion | bytes 2048016 | tf_op jit(solution)/shard_map/jit(dynamic_index_in_dim)/dynamic_slice | solution.py:65
  36.7 0.7 copy.131
  38.2 0.7 copy.125
  38.9 2.8 %copy.145 = bf16[4,250,1000]{1,2,0:T(8,128)(2,1)} copy(bf16[4,250,1000]{2,0,1:T(4,128)(2,1)S(1)} %copy-done.2) | data formatting | bytes 4000000
  41.7 3.0 %fusion.11 = bf16[4,128,4,250]{3,1,2,0:T(8,128)(2,1)S(1)} fusion(bf16[4,250,1000]{1,2,0:T(8,128)(2,1)} %copy.145, bf16[1000,512]{1,0:T(8,128)(2,1)S(1)} %copy-done), kind=kOutput, calls=%fused_computation.9 | convolution fusion | flops 1024512000 | bytes 4048000 | tf_op jit(solution)/shard_map/krs,bsj->bkrj/dot_general | solution.py:54
  44.7 1.0 copy-done.7
  45.7 0.9 dynamic-slice_bitcast_fusion.7
  46.6 2.8 %copy.144 = bf16[4,250,1000]{1,2,0:T(8,128)(2,1)} copy(bf16[4,250,1000]{2,0,1:T(4,128)(2,1)S(1)} %copy-done.1) | data formatting | bytes 4000000
  49.4 3.0 %fusion.8 = bf16[4,128,4,250]{3,1,2,0:T(8,128)(2,1)S(1)} fusion(bf16[4,250,1000]{1,2,0:T(8,128)(2,1)} %copy.144, bf16[1000,512]{1,0:T(8,128)(2,1)S(1)} %copy-done), kind=kOutput, calls=%fused_computation.8 | convolution fusion | flops 1024512000 | bytes 4048000 | tf_op jit(solution)/shard_map/krs,bsj->bkrj/dot_general | solution.py:54
  52.4 1.3 fusion.36
  53.8 1.3 convolution_add_fusion.1
  55.1 2.8 %collective-permute-start.4 = (bf16[4,250,128]{1,2,0:T(8,128)(2,1)}, bf16[4,250,128]{1,2,0:T(8,128)(2,1)}, u32[]{:S(2)}, u32[]{:S(2)}) collective-permute-start(bf16[4,250,128]{1,2,0:T(8,128)(2,1)} %get-tuple-element.15), channel_id=1, source_target_pairs={{0,2},{1,3},{2,0},{3,1},{4,6},{5,7},{6,4},{7,5},{8,10},{9,11},{10,... | collective-permute-start | bytes 768008 | tf_op jit(solution)/shard_map/ppermute | solution.py:64
  57.9 1.3 fusion.44
  59.2 3.0 %collective-permute-start.5 = (bf16[4,250,128]{1,2,0:T(8,128)(2,1)}, bf16[4,250,128]{1,2,0:T(8,128)(2,1)}, u32[]{:S(2)}, u32[]{:S(2)}) collective-permute-start(bf16[4,250,128]{1,2,0:T(8,128)(2,1)} %get-tuple-element.16), channel_id=1, source_target_pairs={{0,3},{1,0},{2,1},{3,2},{4,7},{5,4},{6,5},{7,6},{8,11},{9,8},{10,9... | collective-permute-start | bytes 768008 | tf_op jit(solution)/shard_map/ppermute | solution.py:64
  62.2 2.1 %fusion.28 = bf16[64,4,8,128]{3,2,1,0:T(8,128)(2,1)} fusion(f32[4,128,64,8]{1,3,0,2:T(8,128)S(1)} %fusion.44, f32[4,128,64,8]{1,3,0,2:T(8,128)S(1)} %convolution_add_fusion.1, bf16[4,250,128]{1,2,0:T(8,128)(2,1)} %collective-permute-done.10, bf16[1,250,64,8]{1,3,2,0:T(8,128)(2,1)S(1)} %copy.129), kind=kOutput, calls=%fused_computation.28 | convolution fusion | flops 131858432 | bytes 3133440 | tf_op jit(solution)/shard_map/rpi,krj->pkij/dot_general | solution.py:66
  64.3 12.7 %all-to-all-start.3 = ((bf16[64,4,8,128]{3,2,1,0:T(8,128)(2,1)}), bf16[64,4,8,128]{3,2,1,0:T(8,128)(2,1)S(1)}, u32[]{:S(2)}, u32[]{:S(2)}) async-start(bf16[64,4,8,128]{3,2,1,0:T(8,128)(2,1)} %fusion.28), calls=%async_computation.3 | async-start | bytes 1048576 | tf_op jit(solution)/shard_map/all_to_all | solution.py:70
  77.0 1.3 fusion.38
  78.2 0.9 dynamic-slice_bitcast_fusion.10
  80.2 1.3 fusion.48
  81.5 3.3 %collective-permute-start.2 = (bf16[4,250,128]{1,2,0:T(8,128)(2,1)}, bf16[4,250,128]{1,2,0:T(8,128)(2,1)}, u32[]{:S(2)}, u32[]{:S(2)}) collective-permute-start(bf16[4,250,128]{1,2,0:T(8,128)(2,1)} %get-tuple-element.19), channel_id=1, source_target_pairs={{0,3},{1,0},{2,1},{3,2},{4,7},{5,4},{6,5},{7,6},{8,11},{9,8},{10,9... | collective-permute-start | bytes 768008 | tf_op jit(solution)/shard_map/ppermute | solution.py:64
  84.8 2.1 %fusion.29 = bf16[64,4,8,128]{3,2,1,0:T(8,128)(2,1)} fusion(f32[4,128,64,8]{1,3,0,2:T(8,128)S(1)} %fusion.48, f32[4,128,64,8]{1,3,0,2:T(8,128)S(1)} %convolution_add_fusion.3, bf16[4,250,128]{1,2,0:T(8,128)(2,1)} %collective-permute-done.7, bf16[1,250,64,8]{1,3,2,0:T(8,128)(2,1)S(1)} %copy.129), kind=kOutput, calls=%fused_computation.29 | convolution fusion | flops 131858432 | bytes 3133440 | tf_op jit(solution)/shard_map/rpi,krj->pkij/dot_general | solution.py:66
  86.9 6.3 %all-to-all-done.3.refs_3_ = bf16[64,4,8,128]{3,2,1,0:T(8,128)(2,1)S(1)} async-done(((bf16[64,4,8,128]{3,2,1,0:T(8,128)(2,1)}), bf16[64,4,8,128]{3,2,1,0:T(8,128)(2,1)S(1)}, u32[]{:S(2)}, u32[]{:S(2)}) %all-to-all-start.3) | async-done | bytes 524320 | tf_op jit(solution)/shard_map/all_to_all | solution.py:70
  93.2 5.5 %all-to-all-start.2 = ((bf16[64,4,8,128]{3,2,1,0:T(8,128)(2,1)}), bf16[64,4,8,128]{3,2,1,0:T(8,128)(2,1)S(1)}, u32[]{:S(2)}, u32[]{:S(2)}) async-start(bf16[64,4,8,128]{3,2,1,0:T(8,128)(2,1)} %fusion.29), calls=%async_computation.2 | async-start | bytes 1048576 | tf_op jit(solution)/shard_map/all_to_all | solution.py:70
  98.7 1.3 fusion.40
  100.1 1.3 convolution_add_fusion.5
  101.5 1.3 fusion.52
  102.8 2.1 %fusion.30 = bf16[64,4,8,128]{3,2,1,0:T(8,128)(2,1)} fusion(f32[4,128,64,8]{1,3,0,2:T(8,128)S(1)} %fusion.52, f32[4,128,64,8]{1,3,0,2:T(8,128)S(1)} %convolution_add_fusion.5, bf16[4,250,128]{1,2,0:T(8,128)(2,1)} %collective-permute-done.4, bf16[1,250,64,8]{1,3,2,0:T(8,128)(2,1)S(1)} %copy.129), kind=kOutput, calls=%fused_computation.30 | convolution fusion | flops 131858432 | bytes 3133440 | tf_op jit(solution)/shard_map/rpi,krj->pkij/dot_general | solution.py:66
  104.8 11.3 %all-to-all-done.2.refs_2_ = bf16[64,4,8,128]{3,2,1,0:T(8,128)(2,1)S(1)} async-done(((bf16[64,4,8,128]{3,2,1,0:T(8,128)(2,1)}), bf16[64,4,8,128]{3,2,1,0:T(8,128)(2,1)S(1)}, u32[]{:S(2)}, u32[]{:S(2)}) %all-to-all-start.2) | async-done | bytes 524320 | tf_op jit(solution)/shard_map/all_to_all | solution.py:70
  116.1 5.5 %all-to-all-start.1 = ((bf16[64,4,8,128]{3,2,1,0:T(8,128)(2,1)}), bf16[64,4,8,128]{3,2,1,0:T(8,128)(2,1)S(1)}, u32[]{:S(2)}, u32[]{:S(2)}) async-start(bf16[64,4,8,128]{3,2,1,0:T(8,128)(2,1)} %fusion.30), calls=%async_computation.1 | async-start | bytes 1048576 | tf_op jit(solution)/shard_map/all_to_all | solution.py:70
  121.9 1.3 convolution_add_fusion.7
  123.3 1.3 fusion.59
  124.6 1.3 fusion.31
  125.8 12.3 %all-to-all-done.1.refs_1_ = bf16[64,4,8,128]{3,2,1,0:T(8,128)(2,1)S(1)} async-done(((bf16[64,4,8,128]{3,2,1,0:T(8,128)(2,1)}), bf16[64,4,8,128]{3,2,1,0:T(8,128)(2,1)S(1)}, u32[]{:S(2)}, u32[]{:S(2)}) %all-to-all-start.1) | async-done | bytes 524320 | tf_op jit(solution)/shard_map/all_to_all | solution.py:70
  138.2 21.7 %all_to_all.20.refs_0_ = bf16[64,4,8,128]{3,2,1,0:T(8,128)(2,1)} all-to-all(bf16[64,4,8,128]{3,2,1,0:T(8,128)(2,1)S(1)} %fusion.31), channel_id=1, replica_groups=mesh['pair'=64,'mo'=4] {'pair'}, dimensions={0} | all-to-all | bytes 1048576 | tf_op jit(solution)/shard_map/all_to_all | solution.py:70
  159.8 20.0 %shard_map.37 = f32[1024,8,128]{2,1,0:T(8,128)} custom-call(s32[1024]{0:T(1024)} %mirror_ref.1, bf16[64,4,8,128]{3,2,1,0:T(8,128)(2,1)} %all_to_all.20.refs_0_, bf16[64,4,8,128]{3,2,1,0:T(8,128)(2,1)} %copy-done.11, bf16[64,4,8,128]{3,2,1,0:T(8,128)(2,1)} %copy-done.10, bf16[64,4,8,128]{3,2,1,0:T(8,128)(2,1)} %copy-done.9), custom_call_target="tpu_custom_call" | custom-call | tf_op jit(solution)/shard_map/pallas_call | solution.py:34
  (44 shorter events, 3.6 us)
Async XLA Ops:
  9.5 4.4 %copy-start = (bf16[1000,512]{1,0:T(8,128)(2,1)S(1)}, bf16[1000,512]{1,0:T(8,128)(2,1)}, u32[]{:S(2)}) copy-start(bf16[1000,512]{1,0:T(8,128)(2,1)} %param.4) | copy-start | bytes 3072004
  16.7 1.0 copy-start.8
  18.7 40.5 %collective-permute-start.10 = (bf16[4,250,128]{1,2,0:T(8,128)(2,1)}, bf16[4,250,128]{1,2,0:T(8,128)(2,1)}, u32[]{:S(2)}, u32[]{:S(2)}) collective-permute-start(bf16[4,250,128]{1,2,0:T(8,128)(2,1)} %get-tuple-element.9), channel_id=1, source_target_pairs={{0,2},{1,3},{2,0},{3,1},{4,6},{5,7},{6,4},{7,5},{8,10},{9,11},{10,... | collective-permute-start | bytes 768008 | tf_op jit(solution)/shard_map/ppermute | solution.py:64
  20.8 34.4 %collective-permute-start.11 = (bf16[4,250,128]{1,2,0:T(8,128)(2,1)}, bf16[4,250,128]{1,2,0:T(8,128)(2,1)}, u32[]{:S(2)}, u32[]{:S(2)}) collective-permute-start(bf16[4,250,128]{1,2,0:T(8,128)(2,1)} %get-tuple-element.10), channel_id=1, source_target_pairs={{0,3},{1,0},{2,1},{3,2},{4,7},{5,4},{6,5},{7,6},{8,11},{9,8},{10,9... | collective-permute-start | bytes 768008 | tf_op jit(solution)/shard_map/ppermute | solution.py:64
  21.4 32.3 %collective-permute-start.9 = (bf16[4,250,128]{1,2,0:T(8,128)(2,1)}, bf16[4,250,128]{1,2,0:T(8,128)(2,1)}, u32[]{:S(2)}, u32[]{:S(2)}) collective-permute-start(bf16[4,250,128]{1,2,0:T(8,128)(2,1)} %get-tuple-element.11), channel_id=1, source_target_pairs={{0,1},{1,2},{2,3},{3,0},{4,5},{5,6},{6,7},{7,4},{8,9},{9,10},{10,1... | collective-permute-start | bytes 768008 | tf_op jit(solution)/shard_map/ppermute | solution.py:64
  27.0 1.0 copy-start.6
  29.0 52.6 %collective-permute-start.7 = (bf16[4,250,128]{1,2,0:T(8,128)(2,1)}, bf16[4,250,128]{1,2,0:T(8,128)(2,1)}, u32[]{:S(2)}, u32[]{:S(2)}) collective-permute-start(bf16[4,250,128]{1,2,0:T(8,128)(2,1)} %get-tuple-element.12), channel_id=1, source_target_pairs={{0,2},{1,3},{2,0},{3,1},{4,6},{5,7},{6,4},{7,5},{8,10},{9,11},{10,... | collective-permute-start | bytes 768008 | tf_op jit(solution)/shard_map/ppermute | solution.py:64
  30.3 49.2 %collective-permute-start.8 = (bf16[4,250,128]{1,2,0:T(8,128)(2,1)}, bf16[4,250,128]{1,2,0:T(8,128)(2,1)}, u32[]{:S(2)}, u32[]{:S(2)}) collective-permute-start(bf16[4,250,128]{1,2,0:T(8,128)(2,1)} %get-tuple-element.13), channel_id=1, source_target_pairs={{0,3},{1,0},{2,1},{3,2},{4,7},{5,4},{6,5},{7,6},{8,11},{9,8},{10,9... | collective-permute-start | bytes 768008 | tf_op jit(solution)/shard_map/ppermute | solution.py:64
  36.6 2.3 %copy-start.2 = (bf16[4,250,1000]{2,0,1:T(4,128)(2,1)S(1)}, bf16[4,250,1000]{2,0,1:T(4,128)(2,1)}, u32[]{:S(2)}) copy-start(bf16[4,250,1000]{2,0,1:T(4,128)(2,1)} %get-tuple-element.7) | copy-start | bytes 6000004
  41.7 5.0 %copy-start.1 = (bf16[4,250,1000]{2,0,1:T(4,128)(2,1)S(1)}, bf16[4,250,1000]{2,0,1:T(4,128)(2,1)}, u32[]{:S(2)}) copy-start(bf16[4,250,1000]{2,0,1:T(4,128)(2,1)} %get-tuple-element.8) | copy-start | bytes 6000004
  44.7 1.0 copy-start.7
  49.4 3.0 %copy-start.4 = (bf16[1,250,64,8]{1,3,2,0:T(8,128)(2,1)S(1)}, bf16[1,250,64,8]{1,3,2,0:T(8,128)(2,1)}, u32[]{:S(2)}) copy-start(bf16[1,250,64,8]{1,3,2,0:T(8,128)(2,1)} %copy.125) | copy-start | bytes 768004
  49.4 4.4 %copy-start.3 = (bf16[1,250,64,8]{1,3,2,0:T(8,128)(2,1)S(1)}, bf16[1,250,64,8]{1,3,2,0:T(8,128)(2,1)}, u32[]{:S(2)}) copy-start(bf16[1,250,64,8]{1,3,2,0:T(8,128)(2,1)} %copy.127) | copy-start | bytes 768004
  52.4 5.5 %copy-start.5 = (bf16[1,250,64,8]{1,3,2,0:T(8,128)(2,1)S(1)}, bf16[1,250,64,8]{1,3,2,0:T(8,128)(2,1)}, u32[]{:S(2)}) copy-start(bf16[1,250,64,8]{1,3,2,0:T(8,128)(2,1)} %copy.131) | copy-start | bytes 768004
  53.7 25.5 %collective-permute-start.6 = (bf16[4,250,128]{1,2,0:T(8,128)(2,1)}, bf16[4,250,128]{1,2,0:T(8,128)(2,1)S(1)}, u32[]{:S(2)}, u32[]{:S(2)}) collective-permute-start(bf16[4,250,128]{1,2,0:T(8,128)(2,1)} %get-tuple-element.14), channel_id=1, source_target_pairs={{0,1},{1,2},{2,3},{3,0},{4,5},{5,6},{6,7},{7,4},{8,9},{9,10},{10,1... | collective-permute-start | bytes 768008 | tf_op jit(solution)/shard_map/ppermute | solution.py:64
  55.1 47.6 %collective-permute-start.4 = (bf16[4,250,128]{1,2,0:T(8,128)(2,1)}, bf16[4,250,128]{1,2,0:T(8,128)(2,1)}, u32[]{:S(2)}, u32[]{:S(2)}) collective-permute-start(bf16[4,250,128]{1,2,0:T(8,128)(2,1)} %get-tuple-element.15), channel_id=1, source_target_pairs={{0,2},{1,3},{2,0},{3,1},{4,6},{5,7},{6,4},{7,5},{8,10},{9,11},{10,... | collective-permute-start | bytes 768008 | tf_op jit(solution)/shard_map/ppermute | solution.py:64
  59.2 42.3 %collective-permute-start.5 = (bf16[4,250,128]{1,2,0:T(8,128)(2,1)}, bf16[4,250,128]{1,2,0:T(8,128)(2,1)}, u32[]{:S(2)}, u32[]{:S(2)}) collective-permute-start(bf16[4,250,128]{1,2,0:T(8,128)(2,1)} %get-tuple-element.16), channel_id=1, source_target_pairs={{0,3},{1,0},{2,1},{3,2},{4,7},{5,4},{6,5},{7,6},{8,11},{9,8},{10,9... | collective-permute-start | bytes 768008 | tf_op jit(solution)/shard_map/ppermute | solution.py:64
  64.3 28.9 %all-to-all-start.3 = ((bf16[64,4,8,128]{3,2,1,0:T(8,128)(2,1)}), bf16[64,4,8,128]{3,2,1,0:T(8,128)(2,1)S(1)}, u32[]{:S(2)}, u32[]{:S(2)}) async-start(bf16[64,4,8,128]{3,2,1,0:T(8,128)(2,1)} %fusion.28), calls=%async_computation.3 | async-start | bytes 1048576 | tf_op jit(solution)/shard_map/all_to_all | solution.py:70
  79.2 20.9 %collective-permute-start.3 = (bf16[4,250,128]{1,2,0:T(8,128)(2,1)}, bf16[4,250,128]{1,2,0:T(8,128)(2,1)}, u32[]{:S(2)}, u32[]{:S(2)}) collective-permute-start(bf16[4,250,128]{1,2,0:T(8,128)(2,1)} %get-tuple-element.17), channel_id=1, source_target_pairs={{0,1},{1,2},{2,3},{3,0},{4,5},{5,6},{6,7},{7,4},{8,9},{9,10},{10,1... | collective-permute-start | bytes 768008 | tf_op jit(solution)/shard_map/ppermute | solution.py:64
  79.5 45.0 %collective-permute-start.1 = (bf16[4,250,128]{1,2,0:T(8,128)(2,1)}, bf16[4,250,128]{1,2,0:T(8,128)(2,1)}, u32[]{:S(2)}, u32[]{:S(2)}) collective-permute-start(bf16[4,250,128]{1,2,0:T(8,128)(2,1)} %get-tuple-element.18), channel_id=1, source_target_pairs={{0,2},{1,3},{2,0},{3,1},{4,6},{5,7},{6,4},{7,5},{8,10},{9,11},{10,... | collective-permute-start | bytes 768008 | tf_op jit(solution)/shard_map/ppermute | solution.py:64
  81.5 41.7 %collective-permute-start.2 = (bf16[4,250,128]{1,2,0:T(8,128)(2,1)}, bf16[4,250,128]{1,2,0:T(8,128)(2,1)}, u32[]{:S(2)}, u32[]{:S(2)}) collective-permute-start(bf16[4,250,128]{1,2,0:T(8,128)(2,1)} %get-tuple-element.19), channel_id=1, source_target_pairs={{0,3},{1,0},{2,1},{3,2},{4,7},{5,4},{6,5},{7,6},{8,11},{9,8},{10,9... | collective-permute-start | bytes 768008 | tf_op jit(solution)/shard_map/ppermute | solution.py:64
  93.2 8.2 %copy-start.9 = (bf16[64,4,8,128]{3,2,1,0:T(8,128)(2,1)}, bf16[64,4,8,128]{3,2,1,0:T(8,128)(2,1)S(1)}, u32[]{:S(2)}) copy-start(bf16[64,4,8,128]{3,2,1,0:T(8,128)(2,1)S(1)} %all-to-all-done.3.refs_3_) | copy-start | bytes 1572868
  93.2 22.9 %all-to-all-start.2 = ((bf16[64,4,8,128]{3,2,1,0:T(8,128)(2,1)}), bf16[64,4,8,128]{3,2,1,0:T(8,128)(2,1)S(1)}, u32[]{:S(2)}, u32[]{:S(2)}) async-start(bf16[64,4,8,128]{3,2,1,0:T(8,128)(2,1)} %fusion.29), calls=%async_computation.2 | async-start | bytes 1048576 | tf_op jit(solution)/shard_map/all_to_all | solution.py:70
  100.0 21.9 %collective-permute-start = (bf16[4,250,128]{1,2,0:T(8,128)(2,1)}, bf16[4,250,128]{1,2,0:T(8,128)(2,1)}, u32[]{:S(2)}, u32[]{:S(2)}) collective-permute-start(bf16[4,250,128]{1,2,0:T(8,128)(2,1)} %get-tuple-element.20), channel_id=1, source_target_pairs={{0,1},{1,2},{2,3},{3,0},{4,5},{5,6},{6,7},{7,4},{8,9},{9,10},{10,1... | collective-permute-start | bytes 768008 | tf_op jit(solution)/shard_map/ppermute | solution.py:64
  116.1 7.1 %copy-start.10 = (bf16[64,4,8,128]{3,2,1,0:T(8,128)(2,1)}, bf16[64,4,8,128]{3,2,1,0:T(8,128)(2,1)S(1)}, u32[]{:S(2)}) copy-start(bf16[64,4,8,128]{3,2,1,0:T(8,128)(2,1)S(1)} %all-to-all-done.2.refs_2_) | copy-start | bytes 1572868
  116.1 22.0 %all-to-all-start.1 = ((bf16[64,4,8,128]{3,2,1,0:T(8,128)(2,1)}), bf16[64,4,8,128]{3,2,1,0:T(8,128)(2,1)S(1)}, u32[]{:S(2)}, u32[]{:S(2)}) async-start(bf16[64,4,8,128]{3,2,1,0:T(8,128)(2,1)} %fusion.30), calls=%async_computation.1 | async-start | bytes 1048576 | tf_op jit(solution)/shard_map/all_to_all | solution.py:70
  138.2 21.7 %copy-start.11 = (bf16[64,4,8,128]{3,2,1,0:T(8,128)(2,1)}, bf16[64,4,8,128]{3,2,1,0:T(8,128)(2,1)S(1)}, u32[]{:S(2)}) copy-start(bf16[64,4,8,128]{3,2,1,0:T(8,128)(2,1)S(1)} %all-to-all-done.1.refs_1_) | copy-start | bytes 1572868

commit v4 on v2

v4 whole, which is shorter than its diff:
```python
import functools

import jax
import jax.numpy as jnp
from jax import lax
from jax.experimental import pallas as pl
from jax.experimental.pallas import tpu as pltpu
from jax.sharding import PartitionSpec as P

MESH = pl.DeviceIdType.MESH


def exchange_combine_kernel(n_pair, mirror_ref, x_ref, o_ref, held, send_sems, recv_sems, own_sem):
    me = lax.axis_index("pair")
    mo = lax.axis_index("mo")
    rows = x_ref.shape[1]

    def peer(s):
        return lax.rem(me + s, n_pair)

    barrier = pltpu.get_barrier_semaphore()

    def greet(s, carry):
        pl.semaphore_signal(barrier, 1, device_id=(peer(s), mo), device_id_type=MESH)
        return carry

    lax.fori_loop(1, n_pair, greet, 0)
    pl.semaphore_wait(barrier, n_pair - 1)

    own = pltpu.make_async_copy(x_ref.at[me], held.at[me], own_sem)
    own.start()

    def send(s):
        return pltpu.make_async_remote_copy(
            src_ref=x_ref.at[peer(s)],
            dst_ref=held.at[me],
            send_sem=send_sems.at[s],
            recv_sem=recv_sems.at[s],
            device_id=(peer(s), mo),
            device_id_type=MESH,
        )

    def start(s, carry):
        send(s).start()
        return carry

    def finish(s, carry):
        send(s).wait()
        return carry

    lax.fori_loop(1, n_pair, start, 0)
    own.wait()
    lax.fori_loop(1, n_pair, finish, 0)

    def body(src, carry):
        for kk in range(rows):
            k = src * rows + kk
            m = mirror_ref[k]
            a = held[src, kk].astype(jnp.float32)
            b = held[m // rows, m % rows].astype(jnp.float32)
            o_ref[k] = 0.5 * (a + b)
        return carry

    lax.fori_loop(0, n_pair, body, 0)


def exchange_combine(half, mirror, n_pair):
    _, rows, a, b = half.shape
    return pl.pallas_call(
        functools.partial(exchange_combine_kernel, n_pair),
        out_shape=jax.ShapeDtypeStruct((n_pair * rows, a, b), jnp.float32),
        in_specs=[
            pl.BlockSpec(memory_space=pltpu.SMEM),
            pl.BlockSpec(memory_space=pltpu.VMEM),
        ],
        out_specs=pl.BlockSpec(memory_space=pltpu.VMEM),
        scratch_shapes=[
            pltpu.VMEM(half.shape, half.dtype),
            pltpu.SemaphoreType.DMA((n_pair,)),
            pltpu.SemaphoreType.DMA((n_pair,)),
            pltpu.SemaphoreType.DMA(()),
        ],
        compiler_params=pltpu.CompilerParams(collective_id=0, has_side_effects=True),
    )(mirror, half)


def make_on_device(n_pair, n_mo):
    def on_device(integrals, coeffs, mirror):
        rows, r_loc, nbf = integrals.shape
        nmo = coeffs.shape[1]
        c_j = coeffs.reshape(nbf, n_mo, nmo // n_mo).transpose(1, 0, 2)
        quarter = jnp.einsum(
            "krs,bsj->bkrj", integrals, c_j, preferred_element_type=jnp.float32
        ).astype(jnp.bfloat16)
        arrived = lax.all_to_all(quarter, "mo", 0, 0, tiled=True)
        c_r = coeffs.reshape(n_mo, r_loc, n_pair, nmo // n_pair)
        half = jnp.einsum(
            "brpi,bkrj->pkij", c_r, arrived, preferred_element_type=jnp.float32
        )
        return exchange_combine(half.astype(jnp.bfloat16), mirror, n_pair)

    return on_device


def solution(mesh):
    return jax.shard_map(
        make_on_device(mesh.shape["pair"], mesh.shape["mo"]),
        mesh=mesh,
        in_specs=(P("pair", "mo", None), P(), P()),
        out_specs=P(None, "pair", "mo"),
        check_vma=False,
    )
```

time: 149 us -> 154 us (1.034)
  Pallas kernels: 5.7 us -> 66.5 us
  blocking collectives: 58.6 us -> 0 us
  local copies, waits for them, and re-layouts: 10.5 us -> 13.7 us
    pallas_call x1, Pallas kernels: 5.7 us -> 66.5 us  [exchange_combine(): pl.pallas_call(functools.partial(exchange_combine_kernel, n_pair), out_sh...]
    all_to_all x1 -> x0, blocking collectives: 58.6 us -> none  [on_device(): pieces = lax.all_to_all(half.astype(jnp.bfloat16), 'pair', 0, 0, tiled=True)]
    unnamed x3 -> x4, local copies, waits for them, and re-layouts: 0.53 us -> 5 us
where the time goes in v4:
time: 154 us; the launch traced here: 152 us
  Pallas kernels  66.5 us (43%)
  waiting for transfers between devices  46.2 us (30%)
  matrix products  17.2 us (11%)
  local copies, waits for them, and re-layouts  13.7 us (9%)
  starting transfers between devices  8.16 us (5%)
    pallas_call x1, Pallas kernels, exchange_combine(): pl.pallas_call(functools.partial(exchange_combine_kernel, n_pair), out_sh...  66.5 us
    all_to_all x1, waiting for transfers between devices, on_device(): arrived = lax.all_to_all(quarter, 'mo', 0, 0, tiled=True)  46.2 us
    dot_general x1, matrix products, on_device(): jnp.einsum('krs,bsj->bkrj', integrals, c_j, preferred_element_type=jnp.fl...  11.4 us
    all_to_all x1, starting transfers between devices, on_device(): arrived = lax.all_to_all(quarter, 'mo', 0, 0, tiled=True)  8.16 us
    convert_element_type x1, local copies, waits for them, and re-layouts, on_device(): quarter = jnp.einsum('krs,bsj->bkrj', integrals, c_j, preferred_element_t...  7.55 us
    dot_general x1, matrix products, on_device(): jnp.einsum('brpi,bkrj->pkij', c_r, arrived, preferred_element_type=jnp.fl...  5.89 us
    unnamed x4, local copies, waits for them, and re-layouts  5 us
  transfers between devices with their start and end apart: 1, of which 1 were waited for; matrix products, arithmetic and copies ran while one was open for 1% of the time, Pallas kernels for 0%

profile of v4, /device:TPU:1, one launch (start us, length us, event | category | flops | bytes accessed | tf_op | source)
XLA Modules:
  0.0 151.8 jit_solution(14695771851048594577)
XLA Ops:
  0.0 11.4 %convert_bitcast_fusion = bf16[4,16,250,128]{2,3,0,1:T(8,128)(2,1)} fusion(bf16[16,250,1000,1]{2,0,1,3:T(8,128)(2,1)} %bitcast.30, bf16[1000,512]{1,0:T(8,128)(2,1)} %param.4), kind=kOutput, calls=%fused_computation.6 | convolution fusion | flops 4098048000 | bytes 13120000 | tf_op jit(solution)/shard_map/krs,bsj->bkrj/dot_general | solution.py:92
  11.4 7.6 %copy.11 = bf16[4,16,250,128]{3,1,2,0:T(8,128)(2,1)} copy(bf16[4,16,250,128]{2,3,0,1:T(8,128)(2,1)} %convert_bitcast_fusion) | data formatting | bytes 8192000 | tf_op jit(solution)/shard_map/convert_element_type | solution.py:94
  18.9 0.0 copy-start
  18.9 8.2 %all-to-all-start = ((bf16[4,16,250,128]{3,1,2,0:T(8,128)(2,1)}), bf16[4,16,250,128]{3,1,2,0:T(8,128)(2,1)}, u32[]{:S(2)}, u32[]{:S(2)}) async-start(bf16[4,16,250,128]{3,1,2,0:T(8,128)(2,1)} %copy.11), calls=%async_computation | async-start | bytes 8192000 | tf_op jit(solution)/shard_map/all_to_all | solution.py:95
  27.1 0.0 copy-done
  27.1 0.5 copy.12
  27.6 1.1 reshape.7
  28.7 46.2 %all-to-all-done = bf16[4,16,250,128]{3,1,2,0:T(8,128)(2,1)} async-done(((bf16[4,16,250,128]{3,1,2,0:T(8,128)(2,1)}), bf16[4,16,250,128]{3,1,2,0:T(8,128)(2,1)}, u32[]{:S(2)}, u32[]{:S(2)}) %all-to-all-start) | async-done | bytes 4096032 | tf_op jit(solution)/shard_map/all_to_all | solution.py:95
  74.9 5.9 %fusion.7.x_ref = bf16[64,16,8,128]{3,2,1,0:T(8,128)(2,1)} fusion(bf16[4,16,250,128]{3,1,2,0:T(8,128)(2,1)} %all-to-all-done, bf16[4,250,64,8,1]{1,0,3,2,4:T(4,128)(2,1)S(1)} %bitcast.29), kind=kOutput, calls=%fused_computation.7 | convolution fusion | flops 2098200576 | bytes 7217152 | tf_op jit(solution)/shard_map/brpi,bkrj->pkij/dot_general | solution.py:97
  80.8 66.5 %shard_map.37 = f32[1024,8,128]{2,1,0:T(8,128)} custom-call(s32[1024]{0:T(1024)} %mirror_ref.1, bf16[64,16,8,128]{3,2,1,0:T(8,128)(2,1)} %fusion.7.x_ref), custom_call_target="tpu_custom_call" | custom-call | tf_op jit(solution)/shard_map/pallas_call | solution.py:69
  147.4 4.5 %copy.42 = f32[1024,8,128]{2,1,0:T(8,128)} copy(f32[1024,8,128]{2,1,0:T(8,128)} %shard_map.37) | data formatting | bytes 8388608
Async XLA Ops:
  18.9 8.2 %copy-start = (bf16[1000,512]{1,0:T(8,128)(2,1)S(1)}, bf16[1000,512]{1,0:T(8,128)(2,1)}, u32[]{:S(2)}) copy-start(bf16[1000,512]{1,0:T(8,128)(2,1)} %param.4) | copy-start | bytes 3072004
  18.9 56.0 %all-to-all-start = ((bf16[4,16,250,128]{3,1,2,0:T(8,128)(2,1)}), bf16[4,16,250,128]{3,1,2,0:T(8,128)(2,1)}, u32[]{:S(2)}, u32[]{:S(2)}) async-start(bf16[4,16,250,128]{3,1,2,0:T(8,128)(2,1)} %copy.11), calls=%async_computation | async-start | bytes 8192000 | tf_op jit(solution)/shard_map/all_to_all | solution.py:95

commit v5 on v2

v5 whole, which is shorter than its diff:
```python
import functools

import jax
import jax.numpy as jnp
from jax import lax
from jax.experimental import pallas as pl
from jax.experimental.pallas import tpu as pltpu
from jax.sharding import PartitionSpec as P

MESH = pl.DeviceIdType.MESH
N_CHUNK = 4


def fused_kernel(n_pair, n_mo, n_chunk, mirror_ref, q_ref, ct_ref, o_ref,
                 arrived, sendbuf, held, mo_send, mo_recv, pr_send, pr_recv, own_sem):
    me = lax.axis_index("pair")
    mo = lax.axis_index("mo")
    rows = q_ref.shape[1]
    kc = rows // n_chunk

    def chunk(c):
        return pl.ds(c * kc, kc)

    def mo_copy(c, s):
        b = lax.rem(mo + s, n_mo)
        return pltpu.make_async_remote_copy(
            src_ref=q_ref.at[b, chunk(c)],
            dst_ref=arrived.at[mo, chunk(c)],
            send_sem=mo_send.at[c, s],
            recv_sem=mo_recv.at[c, s],
            device_id=(me, b),
            device_id_type=MESH,
        )

    def pair_copy(c, s):
        p = lax.rem(me + s, n_pair)
        return pltpu.make_async_remote_copy(
            src_ref=sendbuf.at[chunk(c), p],
            dst_ref=held.at[me, chunk(c)],
            send_sem=pr_send.at[c, s],
            recv_sem=pr_recv.at[c, s],
            device_id=(p, mo),
            device_id_type=MESH,
        )

    def own_mo(c):
        return pltpu.make_async_copy(q_ref.at[mo, chunk(c)], arrived.at[mo, chunk(c)], own_sem.at[0, c])

    def own_pair(c):
        return pltpu.make_async_copy(sendbuf.at[chunk(c), me], held.at[me, chunk(c)], own_sem.at[1, c])

    barrier = pltpu.get_barrier_semaphore()

    def greet(s, carry):
        pl.semaphore_signal(barrier, 1, device_id=(lax.rem(me + s, n_pair), mo), device_id_type=MESH)
        return carry

    lax.fori_loop(1, n_pair, greet, 0)
    for s in range(1, n_mo):
        pl.semaphore_signal(barrier, 1, device_id=(me, lax.rem(mo + s, n_mo)), device_id_type=MESH)
    pl.semaphore_wait(barrier, n_pair - 1 + n_mo - 1)

    for c in range(n_chunk):
        own_mo(c).start()
        for s in range(1, n_mo):
            mo_copy(c, s).start()

    for c in range(n_chunk):
        own_mo(c).wait()
        for s in range(1, n_mo):
            mo_copy(c, s).wait()

        def transform(t, carry):
            k = c * kc + t
            acc = jnp.dot(ct_ref[0], arrived[0, k], preferred_element_type=jnp.float32)
            for b in range(1, n_mo):
                acc += jnp.dot(ct_ref[b], arrived[b, k], preferred_element_type=jnp.float32)
            sendbuf[k] = acc.reshape(n_pair, -1, acc.shape[-1]).astype(sendbuf.dtype)
            return carry

        lax.fori_loop(0, kc, transform, 0)
        own_pair(c).start()

        def start(s, carry):
            pair_copy(c, s).start()
            return carry

        lax.fori_loop(1, n_pair, start, 0)

    for c in range(n_chunk):
        own_pair(c).wait()

        def finish(s, carry):
            pair_copy(c, s).wait()
            return carry

        lax.fori_loop(1, n_pair, finish, 0)

    def combine(src, carry):
        for kk in range(rows):
            k = src * rows + kk
            m = mirror_ref[k]
            a = held[src, kk].astype(jnp.float32)
            b = held[m // rows, m % rows].astype(jnp.float32)
            o_ref[k] = 0.5 * (a + b)
        return carry

    lax.fori_loop(0, n_pair, combine, 0)


def fused(quarter, ct, mirror, n_pair):
    n_mo, rows, r_loc, jw = quarter.shape
    nmo = ct.shape[1]
    iw = nmo // n_pair
    return pl.pallas_call(
        functools.partial(fused_kernel, n_pair, n_mo, N_CHUNK),
        out_shape=jax.ShapeDtypeStruct((n_pair * rows, iw, jw), jnp.float32),
        in_specs=[
            pl.BlockSpec(memory_space=pltpu.SMEM),
            pl.BlockSpec(memory_space=pltpu.VMEM),
            pl.BlockSpec(memory_space=pltpu.VMEM),
        ],
        out_specs=pl.BlockSpec(memory_space=pltpu.VMEM),
        scratch_shapes=[
            pltpu.VMEM(quarter.shape, quarter.dtype),
            pltpu.VMEM((rows, n_pair, iw, jw), jnp.bfloat16),
            pltpu.VMEM((n_pair, rows, iw, jw), jnp.bfloat16),
            pltpu.SemaphoreType.DMA((N_CHUNK, n_mo)),
            pltpu.SemaphoreType.DMA((N_CHUNK, n_mo)),
            pltpu.SemaphoreType.DMA((N_CHUNK, n_pair)),
            pltpu.SemaphoreType.DMA((N_CHUNK, n_pair)),
            pltpu.SemaphoreType.DMA((2, N_CHUNK)),
        ],
        compiler_params=pltpu.CompilerParams(
            collective_id=0, has_side_effects=True, vmem_limit_bytes=48 * 1024 * 1024
        ),
    )(mirror, quarter, ct)


def make_on_device(n_pair, n_mo):
    def on_device(integrals, coeffs, mirror):
        rows, r_loc, nbf = integrals.shape
        nmo = coeffs.shape[1]
        c_j = coeffs.reshape(nbf, n_mo, nmo // n_mo).transpose(1, 0, 2)
        quarter = jnp.einsum(
            "krs,bsj->bkrj", integrals, c_j, preferred_element_type=jnp.float32
        ).astype(jnp.bfloat16)
        ct = coeffs.reshape(n_mo, r_loc, nmo).transpose(0, 2, 1)
        return fused(quarter, ct, mirror, n_pair)

    return on_device


def solution(mesh):
    return jax.shard_map(
        make_on_device(mesh.shape["pair"], mesh.shape["mo"]),
        mesh=mesh,
        in_specs=(P("pair", "mo", None), P(), P()),
        out_specs=P(None, "pair", "mo"),
        check_vma=False,
    )
```

time: 149 us -> 119 us (0.80); the launches traced: 146 us -> 119 us
  Pallas kernels: 5.7 us -> 104 us
  blocking collectives: 58.6 us -> 0 us
  waiting for transfers between devices: 46.2 us -> 0 us
  matrix products: 16.9 us -> 8.06 us
  starting transfers between devices: 8.16 us -> 0 us
  local copies, waits for them, and re-layouts: 10.5 us -> 7.13 us
    pallas_call x1, Pallas kernels: 5.7 us -> 104 us  [fused(): pl.pallas_call(functools.partial(fused_kernel, n_pair, n_mo, N_CHUNK), ou...]
    all_to_all x1 -> x0, blocking collectives: 58.6 us -> none  [on_device(): pieces = lax.all_to_all(half.astype(jnp.bfloat16), 'pair', 0, 0, tiled=True)]
    all_to_all x1 -> x0, waiting for transfers between devices: 46.2 us -> none  [on_device(): arrived = lax.all_to_all(quarter, 'mo', 0, 0, tiled=True)]
    all_to_all x1 -> x0, starting transfers between devices: 8.16 us -> none  [on_device(): arrived = lax.all_to_all(quarter, 'mo', 0, 0, tiled=True)]
    dot_general x1 -> x0, matrix products: 5.54 us -> none  [on_device(): jnp.einsum('brpi,bkrj->pkij', c_r, arrived, preferred_element_type=jnp.fl...]
    convert_element_type x1, local copies, waits for them, and re-layouts: 7.55 us -> 3.09 us  [on_device(): quarter = jnp.einsum('krs,bsj->bkrj', integrals, c_j, preferred_element_t...]
    dot_general x1, matrix products: 11.4 us -> 8.06 us  [on_device(): jnp.einsum('krs,bsj->bkrj', integrals, c_j, preferred_element_type=jnp.fl...]
    unnamed x3, local copies, waits for them, and re-layouts: 0.53 us -> 2.02 us
  transfers between devices with their start and end apart: 1 -> 0, of which waited for: 1 -> 0; matrix products, arithmetic and copies ran while one was open for 1% -> 0% of each run, Pallas kernels for 0% -> 0%
where the time goes in v5:
time: 119 us
  Pallas kernels  104 us (87%)
  matrix products  8.06 us (7%)
  local copies, waits for them, and re-layouts  7.13 us (6%)
    pallas_call x1, Pallas kernels, fused(): pl.pallas_call(functools.partial(fused_kernel, n_pair, n_mo, N_CHUNK), ou...  104 us
    dot_general x1, matrix products, on_device(): jnp.einsum('krs,bsj->bkrj', integrals, c_j, preferred_element_type=jnp.fl...  8.06 us
    convert_element_type x1, local copies, waits for them, and re-layouts, on_device(): quarter = jnp.einsum('krs,bsj->bkrj', integrals, c_j, preferred_element_t...  3.09 us

profile of v5, /device:TPU:1, one launch (start us, length us, event | category | flops | bytes accessed | tf_op | source)
XLA Modules:
  0.0 119.3 jit_solution(11753596816944097237)
XLA Ops:
  0.0 1.5 %reshape.7 = bf16[4,250,512]{2,1,0:T(8,128)(2,1)S(1)} reshape(bf16[1000,512]{1,0:T(8,128)(2,1)} %param.4) | data formatting | bytes 2048000 | tf_op jit(solution)/shard_map/reshape | solution.py:148
  1.5 0.5 copy.15
  2.0 8.1 %fusion.2 = bf16[4,128,16,250]{1,2,3,0:T(8,128)(2,1)S(1)} fusion(bf16[16,250,1000]{2,0,1:T(8,128)(2,1)} %param.3, bf16[1000,512]{1,0:T(8,128)(2,1)} %param.4), kind=kOutput, calls=%fused_computation.3 | convolution fusion | flops 4098048000 | bytes 13120000 | tf_op jit(solution)/shard_map/krs,bsj->bkrj/dot_general | solution.py:145
  10.1 0.0 copy-start
  10.1 3.1 %copy.26 = bf16[4,128,16,250]{1,3,2,0:T(8,128)(2,1)} copy(bf16[4,128,16,250]{1,2,3,0:T(8,128)(2,1)S(1)} %fusion.2) | data formatting | bytes 8192000 | tf_op jit(solution)/shard_map/convert_element_type | solution.py:147
  13.2 0.0 copy-done
  13.2 104.1 %shard_map.37 = f32[1024,8,128]{2,1,0:T(8,128)S(1)} custom-call(s32[1024]{0:T(1024)S(1)} %copy-done, bf16[4,16,250,128]{3,2,1,0:T(8,128)(2,1)} %bitcast.24, bf16[4,512,250]{2,1,0:T(8,128)(2,1)S(1)} %bitcast.23), custom_call_target="tpu_custom_call" | custom-call | tf_op jit(solution)/shard_map/pallas_call | solution.py:115
  117.3 2.0 %copy.28 = f32[1024,8,128]{2,1,0:T(8,128)} copy(f32[1024,8,128]{2,1,0:T(8,128)S(1)} %shard_map.37) | data formatting | bytes 8388608
Async XLA Ops:
  10.1 3.1 %copy-start = (s32[1024]{0:T(1024)S(1)}, s32[1024]{0:T(1024)}, u32[]{:S(2)}) copy-start(s32[1024]{0:T(1024)} %mirror_ref.1) | copy-start | bytes 12292

commit v6 on v5

--- a/solution.py
+++ b/solution.py
@@ -8,7 +8,7 @@
 from jax.sharding import PartitionSpec as P
 
 MESH = pl.DeviceIdType.MESH
-N_CHUNK = 4
+N_CHUNK = 8
 
 
 def fused_kernel(n_pair, n_mo, n_chunk, mirror_ref, q_ref, ct_ref, o_ref,

time: 119 us -> 121 us (1.017)
  no operation moved by 1% of the time
where the time goes in v6:
time: 121 us; the launch traced here: 120 us
  Pallas kernels  105 us (87%)
  matrix products  8.06 us (7%)
  local copies, waits for them, and re-layouts  7.13 us (6%)
    pallas_call x1, Pallas kernels, fused(): pl.pallas_call(functools.partial(fused_kernel, n_pair, n_mo, N_CHUNK), ou...  105 us
    dot_general x1, matrix products, on_device(): jnp.einsum('krs,bsj->bkrj', integrals, c_j, preferred_element_type=jnp.fl...  8.06 us
    convert_element_type x1, local copies, waits for them, and re-layouts, on_device(): quarter = jnp.einsum('krs,bsj->bkrj', integrals, c_j, preferred_element_t...  3.09 us

profile of v6, /device:TPU:1, one launch (start us, length us, event | category | flops | bytes accessed | tf_op | source)
XLA Modules:
  0.0 120.4 jit_solution(11342522275017766941)
XLA Ops:
  0.0 1.5 %reshape.7 = bf16[4,250,512]{2,1,0:T(8,128)(2,1)S(1)} reshape(bf16[1000,512]{1,0:T(8,128)(2,1)} %param.4) | data formatting | bytes 2048000 | tf_op jit(solution)/shard_map/reshape | solution.py:148
  1.5 0.5 copy.15
  2.0 8.1 %fusion.2 = bf16[4,128,16,250]{1,2,3,0:T(8,128)(2,1)S(1)} fusion(bf16[16,250,1000]{2,0,1:T(8,128)(2,1)} %param.3, bf16[1000,512]{1,0:T(8,128)(2,1)} %param.4), kind=kOutput, calls=%fused_computation.3 | convolution fusion | flops 4098048000 | bytes 13120000 | tf_op jit(solution)/shard_map/krs,bsj->bkrj/dot_general | solution.py:145
  10.1 0.0 copy-start
  10.1 3.1 %copy.26 = bf16[4,128,16,250]{1,3,2,0:T(8,128)(2,1)} copy(bf16[4,128,16,250]{1,2,3,0:T(8,128)(2,1)S(1)} %fusion.2) | data formatting | bytes 8192000 | tf_op jit(solution)/shard_map/convert_element_type | solution.py:147
  13.2 0.0 copy-done
  13.2 105.1 %shard_map.37 = f32[1024,8,128]{2,1,0:T(8,128)S(1)} custom-call(s32[1024]{0:T(1024)S(1)} %copy-done, bf16[4,16,250,128]{3,2,1,0:T(8,128)(2,1)} %bitcast.24, bf16[4,512,250]{2,1,0:T(8,128)(2,1)S(1)} %bitcast.23), custom_call_target="tpu_custom_call" | custom-call | tf_op jit(solution)/shard_map/pallas_call | solution.py:115
  118.3 2.0 %copy.28 = f32[1024,8,128]{2,1,0:T(8,128)} copy(f32[1024,8,128]{2,1,0:T(8,128)S(1)} %shard_map.37) | data formatting | bytes 8388608
Async XLA Ops:
  10.1 3.1 %copy-start = (s32[1024]{0:T(1024)S(1)}, s32[1024]{0:T(1024)}, u32[]{:S(2)}) copy-start(s32[1024]{0:T(1024)} %mirror_ref.1) | copy-start | bytes 12292

commit v7 on v5

--- a/solution.py
+++ b/solution.py
@@ -11,8 +11,8 @@
 N_CHUNK = 4
 
 
-def fused_kernel(n_pair, n_mo, n_chunk, mirror_ref, q_ref, ct_ref, o_ref,
-                 arrived, sendbuf, held, mo_send, mo_recv, pr_send, pr_recv, own_sem):
+def fused_kernel(n_pair, n_mo, n_chunk, mirror_ref, x_ref, c_ref, ct_ref, o_ref,
+                 q_ref, arrived, sendbuf, held, mo_send, mo_recv, pr_send, pr_recv, own_sem):
     me = lax.axis_index("pair")
     mo = lax.axis_index("mo")
     rows = q_ref.shape[1]
@@ -60,7 +60,18 @@
         pl.semaphore_signal(barrier, 1, device_id=(me, lax.rem(mo + s, n_mo)), device_id_type=MESH)
     pl.semaphore_wait(barrier, n_pair - 1 + n_mo - 1)
 
+    jw = q_ref.shape[-1]
     for c in range(n_chunk):
+
+        def first(t, carry):
+            k = c * kc + t
+            res = jnp.dot(x_ref[k], c_ref[...], preferred_element_type=jnp.float32)
+            res = res.astype(q_ref.dtype)
+            for b in range(n_mo):
+                q_ref[b, k] = res[:, b * jw:(b + 1) * jw]
+            return carry
+
+        lax.fori_loop(0, kc, first, 0)
         own_mo(c).start()
         for s in range(1, n_mo):
             mo_copy(c, s).start()
@@ -108,21 +119,19 @@
     lax.fori_loop(0, n_pair, combine, 0)
 
 
-def fused(quarter, ct, mirror, n_pair):
-    n_mo, rows, r_loc, jw = quarter.shape
-    nmo = ct.shape[1]
-    iw = nmo // n_pair
+def fused(integrals, coeffs, ct, mirror, n_pair, n_mo):
+    rows, r_loc, _ = integrals.shape
+    nmo = coeffs.shape[1]
+    iw, jw = nmo // n_pair, nmo // n_mo
     return pl.pallas_call(
         functools.partial(fused_kernel, n_pair, n_mo, N_CHUNK),
         out_shape=jax.ShapeDtypeStruct((n_pair * rows, iw, jw), jnp.float32),
-        in_specs=[
-            pl.BlockSpec(memory_space=pltpu.SMEM),
-            pl.BlockSpec(memory_space=pltpu.VMEM),
-            pl.BlockSpec(memory_space=pltpu.VMEM),
-        ],
+        in_specs=[pl.BlockSpec(memory_space=pltpu.SMEM)]
+        + [pl.BlockSpec(memory_space=pltpu.VMEM)] * 3,
         out_specs=pl.BlockSpec(memory_space=pltpu.VMEM),
         scratch_shapes=[
-            pltpu.VMEM(quarter.shape, quarter.dtype),
+            pltpu.VMEM((n_mo, rows, r_loc, jw), jnp.bfloat16),
+            pltpu.VMEM((n_mo, rows, r_loc, jw), jnp.bfloat16),
             pltpu.VMEM((rows, n_pair, iw, jw), jnp.bfloat16),
             pltpu.VMEM((n_pair, rows, iw, jw), jnp.bfloat16),
             pltpu.SemaphoreType.DMA((N_CHUNK, n_mo)),
@@ -132,21 +141,17 @@
             pltpu.SemaphoreType.DMA((2, N_CHUNK)),
         ],
         compiler_params=pltpu.CompilerParams(
-            collective_id=0, has_side_effects=True, vmem_limit_bytes=48 * 1024 * 1024
+            collective_id=0, has_side_effects=True, vmem_limit_bytes=60 * 1024 * 1024
         ),
-    )(mirror, quarter, ct)
+    )(mirror, integrals, coeffs, ct)
 
 
 def make_on_device(n_pair, n_mo):
     def on_device(integrals, coeffs, mirror):
         rows, r_loc, nbf = integrals.shape
         nmo = coeffs.shape[1]
-        c_j = coeffs.reshape(nbf, n_mo, nmo // n_mo).transpose(1, 0, 2)
-        quarter = jnp.einsum(
-            "krs,bsj->bkrj", integrals, c_j, preferred_element_type=jnp.float32
-        ).astype(jnp.bfloat16)
         ct = coeffs.reshape(n_mo, r_loc, nmo).transpose(0, 2, 1)
-        return fused(quarter, ct, mirror, n_pair)
+        return fused(integrals, coeffs, ct, mirror, n_pair, n_mo)
 
     return on_device
 

time: 119 us -> 128 us (1.076)
  local copies, waits for them, and re-layouts: 7.13 us -> 18.4 us
  matrix products: 8.06 us -> 0 us
  Pallas kernels: 104 us -> 110 us
    unnamed x3 -> x2, local copies, waits for them, and re-layouts: 2.02 us -> 15.6 us
    dot_general x1 -> x0, matrix products: 8.06 us -> none  [on_device(): jnp.einsum('krs,bsj->bkrj', integrals, c_j, preferred_element_type=jnp.fl...]
    pallas_call x1, Pallas kernels: 104 us -> 110 us  [fused(): pl.pallas_call(functools.partial(fused_kernel, n_pair, n_mo, N_CHUNK), ou...]
    convert_element_type x1 -> x0, local copies, waits for them, and re-layouts: 3.09 us -> none  [on_device(): quarter = jnp.einsum('krs,bsj->bkrj', integrals, c_j, preferred_element_t...]
where the time goes in v7:
time: 128 us
  Pallas kernels  110 us (86%)
  local copies, waits for them, and re-layouts  18.4 us (14%)
    pallas_call x1, Pallas kernels, fused(): pl.pallas_call(functools.partial(fused_kernel, n_pair, n_mo, N_CHUNK), ou...  110 us
    unnamed x2, local copies, waits for them, and re-layouts  15.6 us
    reshape x2, local copies, waits for them, and re-layouts, on_device(): ct = coeffs.reshape(n_mo, r_loc, nmo).transpose(0, 2, 1)  2.8 us

profile of v7, /device:TPU:1, one launch (start us, length us, event | category | flops | bytes accessed | tf_op | source)
XLA Modules:
  0.0 128.0 jit_solution(2462001906519696708)
XLA Ops:
  0.0 1.5 %reshape.3 = bf16[4,250,512]{2,1,0:T(8,128)(2,1)S(1)} reshape(bf16[1000,512]{1,0:T(8,128)(2,1)} %c_ref.1) | data formatting | bytes 2048000 | tf_op jit(solution)/shard_map/reshape | solution.py:153
  1.5 1.3 %copy.5 = bf16[4,250,512]{1,2,0:T(8,128)(2,1)} copy(bf16[4,250,512]{2,1,0:T(8,128)(2,1)S(1)} %reshape.3) | data formatting | bytes 2048000 | tf_op jit(solution)/shard_map/reshape | solution.py:153
  2.8 11.2 %copy.6.x_ref = bf16[16,250,1000]{2,1,0:T(8,128)(2,1)} copy(bf16[16,250,1000]{2,0,1:T(8,128)(2,1)} %param.3) | data formatting | bytes 16000000 | tf_op args[0]
  14.0 109.5 %shard_map.37 = f32[1024,8,128]{2,1,0:T(8,128)} custom-call(s32[1024]{0:T(1024)} %mirror_ref.1, bf16[16,250,1000]{2,1,0:T(8,128)(2,1)} %copy.6.x_ref, bf16[1000,512]{1,0:T(8,128)(2,1)} %c_ref.1, bf16[4,512,250]{2,1,0:T(8,128)(2,1)} %bitcast.1), custom_call_target="tpu_custom_call" | custom-call | tf_op jit(solution)/shard_map/pallas_call | solution.py:126
  123.5 4.5 %copy.8 = f32[1024,8,128]{2,1,0:T(8,128)} copy(f32[1024,8,128]{2,1,0:T(8,128)} %shard_map.37) | data formatting | bytes 8388608

commit v8 on v5

--- a/solution.py
+++ b/solution.py
@@ -25,7 +25,7 @@
         b = lax.rem(mo + s, n_mo)
         return pltpu.make_async_remote_copy(
             src_ref=q_ref.at[b, chunk(c)],
-            dst_ref=arrived.at[mo, chunk(c)],
+            dst_ref=arrived.at[chunk(c), mo],
             send_sem=mo_send.at[c, s],
             recv_sem=mo_recv.at[c, s],
             device_id=(me, b),
@@ -44,7 +44,7 @@
         )
 
     def own_mo(c):
-        return pltpu.make_async_copy(q_ref.at[mo, chunk(c)], arrived.at[mo, chunk(c)], own_sem.at[0, c])
+        return pltpu.make_async_copy(q_ref.at[mo, chunk(c)], arrived.at[chunk(c), mo], own_sem.at[0, c])
 
     def own_pair(c):
         return pltpu.make_async_copy(sendbuf.at[chunk(c), me], held.at[me, chunk(c)], own_sem.at[1, c])
@@ -72,9 +72,9 @@
 
         def transform(t, carry):
             k = c * kc + t
-            acc = jnp.dot(ct_ref[0], arrived[0, k], preferred_element_type=jnp.float32)
-            for b in range(1, n_mo):
-                acc += jnp.dot(ct_ref[b], arrived[b, k], preferred_element_type=jnp.float32)
+            block = arrived[k]
+            block = block.reshape(-1, block.shape[-1])
+            acc = jnp.dot(ct_ref[...], block, preferred_element_type=jnp.float32)
             sendbuf[k] = acc.reshape(n_pair, -1, acc.shape[-1]).astype(sendbuf.dtype)
             return carry
 
@@ -108,10 +108,14 @@
     lax.fori_loop(0, n_pair, combine, 0)
 
 
-def fused(quarter, ct, mirror, n_pair):
+def fused(quarter, coeffs, mirror, n_pair):
     n_mo, rows, r_loc, jw = quarter.shape
-    nmo = ct.shape[1]
+    nmo = coeffs.shape[1]
     iw = nmo // n_pair
+    r_pad = -(-r_loc // 16) * 16
+    quarter = jnp.pad(quarter, ((0, 0), (0, 0), (0, r_pad - r_loc), (0, 0)))
+    ct = coeffs.reshape(n_mo, r_loc, nmo)
+    ct = jnp.pad(ct, ((0, 0), (0, r_pad - r_loc), (0, 0))).reshape(n_mo * r_pad, nmo).T
     return pl.pallas_call(
         functools.partial(fused_kernel, n_pair, n_mo, N_CHUNK),
         out_shape=jax.ShapeDtypeStruct((n_pair * rows, iw, jw), jnp.float32),
@@ -122,7 +126,7 @@
         ],
         out_specs=pl.BlockSpec(memory_space=pltpu.VMEM),
         scratch_shapes=[
-            pltpu.VMEM(quarter.shape, quarter.dtype),
+            pltpu.VMEM((rows, n_mo, r_pad, jw), quarter.dtype),
             pltpu.VMEM((rows, n_pair, iw, jw), jnp.bfloat16),
             pltpu.VMEM((n_pair, rows, iw, jw), jnp.bfloat16),
             pltpu.SemaphoreType.DMA((N_CHUNK, n_mo)),
@@ -145,8 +149,7 @@
         quarter = jnp.einsum(
             "krs,bsj->bkrj", integrals, c_j, preferred_element_type=jnp.float32
         ).astype(jnp.bfloat16)
-        ct = coeffs.reshape(n_mo, r_loc, nmo).transpose(0, 2, 1)
-        return fused(quarter, ct, mirror, n_pair)
+        return fused(quarter, coeffs, mirror, n_pair)
 
     return on_device
 

time: 119 us -> 120 us (level)
    pad x0 -> x2, local copies, waits for them, and re-layouts: none -> 2.42 us  [the longest x1 2.33 us: fused(): quarter = jnp.pad(quarter, ((0, 0), (0, 0), (0, r_pad - r_loc), (0, 0)))]
    convert_element_type x1, local copies, waits for them, and re-layouts: 3.09 us -> 1.07 us  [on_device(): quarter = jnp.einsum('krs,bsj->bkrj', integrals, c_j, preferred_element_t...]
where the time goes in v8:
time: 120 us
  Pallas kernels  104 us (87%)
  matrix products  7.94 us (7%)
  local copies, waits for them, and re-layouts  7.62 us (6%)
    pallas_call x1, Pallas kernels, fused(): pl.pallas_call(functools.partial(fused_kernel, n_pair, n_mo, N_CHUNK), ou...  104 us
    dot_general x1, matrix products, on_device(): jnp.einsum('krs,bsj->bkrj', integrals, c_j, preferred_element_type=jnp.fl...  7.94 us

profile of v8, /device:TPU:1, one launch (start us, length us, event | category | flops | bytes accessed | tf_op | source)
XLA Modules:
  0.0 119.7 jit_solution(1805530945791543020)
XLA Ops:
  0.0 0.0 copy-start.1
  0.0 1.6 %reshape.10 = bf16[4,250,512]{2,1,0:T(8,128)(2,1)S(1)} reshape(bf16[1000,512]{1,0:T(8,128)(2,1)} %param.4) | data formatting | bytes 2048000 | tf_op jit(solution)/shard_map/reshape | solution.py:117
  1.6 0.1 pad.9
  1.7 0.5 copy.21
  2.2 0.0 copy-done.1
  2.2 7.9 %fusion.2 = bf16[4,128,16,250]{1,2,3,0:T(8,128)(2,1)S(1)} fusion(bf16[16,250,1000]{2,0,1:T(8,128)(2,1)} %param.3, bf16[1000,512]{1,0:T(8,128)(2,1)S(1)} %copy-done.1), kind=kOutput, calls=%fused_computation.3 | convolution fusion | flops 4098048000 | bytes 13120000 | tf_op jit(solution)/shard_map/krs,bsj->bkrj/dot_general | solution.py:149
  10.2 1.1 copy.28
  11.3 0.0 copy-start
  11.3 2.3 %pad.8.q_ref = bf16[4,16,256,128]{3,2,1,0:T(8,128)(2,1)} pad(bf16[4,16,250,128]{3,2,1,0:T(8,128)(2,1)S(1)} %bitcast.25, bf16[]{:T(256)} %constant.2.clone.1), padding=0_0x0_0x0_6x0_0 | pad | bytes 8290306 | tf_op jit(solution)/shard_map/jit(_pad)/pad | solution.py:116
  13.6 0.0 copy-done
  13.6 104.1 %shard_map.37 = f32[1024,8,128]{2,1,0:T(8,128)S(1)} custom-call(s32[1024]{0:T(1024)S(1)} %copy-done, bf16[4,16,256,128]{3,2,1,0:T(8,128)(2,1)} %pad.8.q_ref, bf16[512,1024]{1,0:T(8,128)(2,1)S(1)} %bitcast.24), custom_call_target="tpu_custom_call" | custom-call | tf_op jit(solution)/shard_map/pallas_call | solution.py:119
  117.7 2.0 %copy.30 = f32[1024,8,128]{2,1,0:T(8,128)} copy(f32[1024,8,128]{2,1,0:T(8,128)S(1)} %shard_map.37) | data formatting | bytes 8388608
Async XLA Ops:
  0.0 2.2 %copy-start.1 = (bf16[1000,512]{1,0:T(8,128)(2,1)S(1)}, bf16[1000,512]{1,0:T(8,128)(2,1)}, u32[]{:S(2)}) copy-start(bf16[1000,512]{1,0:T(8,128)(2,1)} %param.4) | copy-start | bytes 3072004
  11.3 2.3 %copy-start = (s32[1024]{0:T(1024)S(1)}, s32[1024]{0:T(1024)}, u32[]{:S(2)}) copy-start(s32[1024]{0:T(1024)} %mirror_ref.1) | copy-start | bytes 12292

commit v9 on v8

--- a/solution.py
+++ b/solution.py
@@ -9,6 +9,7 @@
 
 MESH = pl.DeviceIdType.MESH
 N_CHUNK = 4
+MO_AHEAD = 2
 
 
 def fused_kernel(n_pair, n_mo, n_chunk, mirror_ref, q_ref, ct_ref, o_ref,
@@ -60,10 +61,13 @@
         pl.semaphore_signal(barrier, 1, device_id=(me, lax.rem(mo + s, n_mo)), device_id_type=MESH)
     pl.semaphore_wait(barrier, n_pair - 1 + n_mo - 1)
 
-    for c in range(n_chunk):
+    def start_mo(c):
         own_mo(c).start()
         for s in range(1, n_mo):
             mo_copy(c, s).start()
+
+    for c in range(min(MO_AHEAD, n_chunk)):
+        start_mo(c)
 
     for c in range(n_chunk):
         own_mo(c).wait()
@@ -86,6 +90,8 @@
             return carry
 
         lax.fori_loop(1, n_pair, start, 0)
+        if c + MO_AHEAD < n_chunk:
+            start_mo(c + MO_AHEAD)
 
     for c in range(n_chunk):
         own_pair(c).wait()

time: 120 us -> 120 us (level)
  no operation moved by 1% of the time
where the time goes in v9:
time: 120 us
  Pallas kernels  104 us (87%)
  matrix products  7.94 us (7%)
  local copies, waits for them, and re-layouts  7.62 us (6%)
    pallas_call x1, Pallas kernels, fused(): pl.pallas_call(functools.partial(fused_kernel, n_pair, n_mo, N_CHUNK), ou...  104 us
    dot_general x1, matrix products, on_device(): jnp.einsum('krs,bsj->bkrj', integrals, c_j, preferred_element_type=jnp.fl...  7.94 us

profile of v9, /device:TPU:1, one launch (start us, length us, event | category | flops | bytes accessed | tf_op | source)
XLA Modules:
  0.0 119.8 jit_solution(393795205110281638)
XLA Ops:
  0.0 0.0 copy-start.1
  0.0 1.6 %reshape.10 = bf16[4,250,512]{2,1,0:T(8,128)(2,1)S(1)} reshape(bf16[1000,512]{1,0:T(8,128)(2,1)} %param.4) | data formatting | bytes 2048000 | tf_op jit(solution)/shard_map/reshape | solution.py:123
  1.6 0.1 pad.9
  1.7 0.5 copy.21
  2.2 0.0 copy-done.1
  2.2 7.9 %fusion.2 = bf16[4,128,16,250]{1,2,3,0:T(8,128)(2,1)S(1)} fusion(bf16[16,250,1000]{2,0,1:T(8,128)(2,1)} %param.3, bf16[1000,512]{1,0:T(8,128)(2,1)S(1)} %copy-done.1), kind=kOutput, calls=%fused_computation.3 | convolution fusion | flops 4098048000 | bytes 13120000 | tf_op jit(solution)/shard_map/krs,bsj->bkrj/dot_general | solution.py:155
  10.2 1.1 copy.28
  11.3 0.0 copy-start
  11.3 2.3 %pad.8.q_ref = bf16[4,16,256,128]{3,2,1,0:T(8,128)(2,1)} pad(bf16[4,16,250,128]{3,2,1,0:T(8,128)(2,1)S(1)} %bitcast.25, bf16[]{:T(256)} %constant.2.clone.1), padding=0_0x0_0x0_6x0_0 | pad | bytes 8290306 | tf_op jit(solution)/shard_map/jit(_pad)/pad | solution.py:122
  13.6 0.0 copy-done
  13.6 104.2 %shard_map.37 = f32[1024,8,128]{2,1,0:T(8,128)S(1)} custom-call(s32[1024]{0:T(1024)S(1)} %copy-done, bf16[4,16,256,128]{3,2,1,0:T(8,128)(2,1)} %pad.8.q_ref, bf16[512,1024]{1,0:T(8,128)(2,1)S(1)} %bitcast.24), custom_call_target="tpu_custom_call" | custom-call | tf_op jit(solution)/shard_map/pallas_call | solution.py:125
  117.8 2.0 %copy.30 = f32[1024,8,128]{2,1,0:T(8,128)} copy(f32[1024,8,128]{2,1,0:T(8,128)S(1)} %shard_map.37) | data formatting | bytes 8388608
Async XLA Ops:
  0.0 2.2 %copy-start.1 = (bf16[1000,512]{1,0:T(8,128)(2,1)S(1)}, bf16[1000,512]{1,0:T(8,128)(2,1)}, u32[]{:S(2)}) copy-start(bf16[1000,512]{1,0:T(8,128)(2,1)} %param.4) | copy-start | bytes 3072004
  11.3 2.3 %copy-start = (s32[1024]{0:T(1024)S(1)}, s32[1024]{0:T(1024)}, u32[]{:S(2)}) copy-start(s32[1024]{0:T(1024)} %mirror_ref.1) | copy-start | bytes 12292

commit v10 on v7

--- a/solution.py
+++ b/solution.py
@@ -63,15 +63,12 @@
     jw = q_ref.shape[-1]
     for c in range(n_chunk):
 
-        def first(t, carry):
+        for t in range(kc):
             k = c * kc + t
-            res = jnp.dot(x_ref[k], c_ref[...], preferred_element_type=jnp.float32)
+            res = jnp.dot(x_ref[:, k, :], c_ref[...], preferred_element_type=jnp.float32)
             res = res.astype(q_ref.dtype)
             for b in range(n_mo):
                 q_ref[b, k] = res[:, b * jw:(b + 1) * jw]
-            return carry
-
-        lax.fori_loop(0, kc, first, 0)
         own_mo(c).start()
         for s in range(1, n_mo):
             mo_copy(c, s).start()
@@ -121,6 +118,7 @@
 
 def fused(integrals, coeffs, ct, mirror, n_pair, n_mo):
     rows, r_loc, _ = integrals.shape
+    integrals = integrals.transpose(1, 0, 2)
     nmo = coeffs.shape[1]
     iw, jw = nmo // n_pair, nmo // n_mo
     return pl.pallas_call(

time: 128 us -> 118 us (0.922)
  local copies, waits for them, and re-layouts: 18.4 us -> 7.27 us
    unnamed x2 -> x1, local copies, waits for them, and re-layouts: 15.6 us -> 4.47 us
    pallas_call x1, Pallas kernels: 110 us -> 111 us  [fused(): pl.pallas_call(functools.partial(fused_kernel, n_pair, n_mo, N_CHUNK), ou...]
where the time goes in v10:
time: 118 us
  Pallas kernels  111 us (94%)
  local copies, waits for them, and re-layouts  7.27 us (6%)
    pallas_call x1, Pallas kernels, fused(): pl.pallas_call(functools.partial(fused_kernel, n_pair, n_mo, N_CHUNK), ou...  111 us
    unnamed x1, local copies, waits for them, and re-layouts  4.47 us
    reshape x2, local copies, waits for them, and re-layouts, on_device(): ct = coeffs.reshape(n_mo, r_loc, nmo).transpose(0, 2, 1)  2.8 us

profile of v10, /device:TPU:1, one launch (start us, length us, event | category | flops | bytes accessed | tf_op | source)
XLA Modules:
  0.0 118.1 jit_solution(3226471709794326032)
XLA Ops:
  0.0 1.5 %reshape.3 = bf16[4,250,512]{2,1,0:T(8,128)(2,1)S(1)} reshape(bf16[1000,512]{1,0:T(8,128)(2,1)} %c_ref.1) | data formatting | bytes 2048000 | tf_op jit(solution)/shard_map/reshape | solution.py:151
  1.5 1.3 %copy.4 = bf16[4,250,512]{1,2,0:T(8,128)(2,1)} copy(bf16[4,250,512]{2,1,0:T(8,128)(2,1)S(1)} %reshape.3) | data formatting | bytes 2048000 | tf_op jit(solution)/shard_map/reshape | solution.py:151
  2.8 110.8 %shard_map.37 = f32[1024,8,128]{2,1,0:T(8,128)} custom-call(s32[1024]{0:T(1024)} %mirror_ref.1, bf16[250,16,1000]{2,1,0:T(8,128)(2,1)} %bitcast.2, bf16[1000,512]{1,0:T(8,128)(2,1)} %c_ref.1, bf16[4,512,250]{2,1,0:T(8,128)(2,1)} %bitcast.3), custom_call_target="tpu_custom_call" | custom-call | tf_op jit(solution)/shard_map/pallas_call | solution.py:124
  113.6 4.5 %copy.6 = f32[1024,8,128]{2,1,0:T(8,128)} copy(f32[1024,8,128]{2,1,0:T(8,128)} %shard_map.37) | data formatting | bytes 8388608

commit v11 on v10

--- a/solution.py
+++ b/solution.py
@@ -11,8 +11,8 @@
 N_CHUNK = 4
 
 
-def fused_kernel(n_pair, n_mo, n_chunk, mirror_ref, x_ref, c_ref, ct_ref, o_ref,
-                 q_ref, arrived, sendbuf, held, mo_send, mo_recv, pr_send, pr_recv, own_sem):
+def fused_kernel(n_pair, n_mo, n_chunk, x_ref, c_ref, ct_ref, held,
+                 q_ref, arrived, sendbuf, mo_send, mo_recv, pr_send, pr_recv, own_sem):
     me = lax.axis_index("pair")
     mo = lax.axis_index("mo")
     rows = q_ref.shape[1]
@@ -104,34 +104,21 @@
 
         lax.fori_loop(1, n_pair, finish, 0)
 
-    def combine(src, carry):
-        for kk in range(rows):
-            k = src * rows + kk
-            m = mirror_ref[k]
-            a = held[src, kk].astype(jnp.float32)
-            b = held[m // rows, m % rows].astype(jnp.float32)
-            o_ref[k] = 0.5 * (a + b)
-        return carry
 
-    lax.fori_loop(0, n_pair, combine, 0)
-
-
-def fused(integrals, coeffs, ct, mirror, n_pair, n_mo):
+def fused(integrals, coeffs, ct, n_pair, n_mo):
     rows, r_loc, _ = integrals.shape
     integrals = integrals.transpose(1, 0, 2)
     nmo = coeffs.shape[1]
     iw, jw = nmo // n_pair, nmo // n_mo
     return pl.pallas_call(
         functools.partial(fused_kernel, n_pair, n_mo, N_CHUNK),
-        out_shape=jax.ShapeDtypeStruct((n_pair * rows, iw, jw), jnp.float32),
-        in_specs=[pl.BlockSpec(memory_space=pltpu.SMEM)]
-        + [pl.BlockSpec(memory_space=pltpu.VMEM)] * 3,
+        out_shape=jax.ShapeDtypeStruct((n_pair, rows, iw, jw), jnp.bfloat16),
+        in_specs=[pl.BlockSpec(memory_space=pltpu.VMEM)] * 3,
         out_specs=pl.BlockSpec(memory_space=pltpu.VMEM),
         scratch_shapes=[
             pltpu.VMEM((n_mo, rows, r_loc, jw), jnp.bfloat16),
             pltpu.VMEM((n_mo, rows, r_loc, jw), jnp.bfloat16),
             pltpu.VMEM((rows, n_pair, iw, jw), jnp.bfloat16),
-            pltpu.VMEM((n_pair, rows, iw, jw), jnp.bfloat16),
             pltpu.SemaphoreType.DMA((N_CHUNK, n_mo)),
             pltpu.SemaphoreType.DMA((N_CHUNK, n_mo)),
             pltpu.SemaphoreType.DMA((N_CHUNK, n_pair)),
@@ -141,7 +128,29 @@
         compiler_params=pltpu.CompilerParams(
             collective_id=0, has_side_effects=True, vmem_limit_bytes=60 * 1024 * 1024
         ),
-    )(mirror, integrals, coeffs, ct)
+    )(integrals, coeffs, ct)
+
+
+def combine_kernel(mirror_ref, x_ref, o_ref):
+    def body(k, carry):
+        a = x_ref[k].astype(jnp.float32)
+        b = x_ref[mirror_ref[k]].astype(jnp.float32)
+        o_ref[k] = 0.5 * (a + b)
+        return carry
+
+    lax.fori_loop(0, x_ref.shape[0], body, 0, unroll=8)
+
+
+def combine(pieces, mirror):
+    return pl.pallas_call(
+        combine_kernel,
+        out_shape=jax.ShapeDtypeStruct(pieces.shape, jnp.float32),
+        in_specs=[
+            pl.BlockSpec(memory_space=pltpu.SMEM),
+            pl.BlockSpec(memory_space=pltpu.VMEM),
+        ],
+        out_specs=pl.BlockSpec(memory_space=pltpu.VMEM),
+    )(mirror, pieces)
 
 
 def make_on_device(n_pair, n_mo):
@@ -149,7 +158,8 @@
         rows, r_loc, nbf = integrals.shape
         nmo = coeffs.shape[1]
         ct = coeffs.reshape(n_mo, r_loc, nmo).transpose(0, 2, 1)
-        return fused(integrals, coeffs, ct, mirror, n_pair, n_mo)
+        held = fused(integrals, coeffs, ct, n_pair, n_mo)
+        return combine(held.reshape(-1, *held.shape[2:]), mirror)
 
     return on_device
 

time: 118 us -> 111 us (0.941)
  local copies, waits for them, and re-layouts: 7.27 us -> 2.8 us
  Pallas kernels: 111 us -> 108 us
    pallas_call x1, Pallas kernels: 111 us -> 103 us  [fused(): pl.pallas_call(functools.partial(fused_kernel, n_pair, n_mo, N_CHUNK), ou...]
    pallas_call x0 -> x1, Pallas kernels: none -> 5.7 us  [combine(): pl.pallas_call(combine_kernel, out_shape=jax.ShapeDtypeStruct(pieces.shap...]
    unnamed x1 -> x0, local copies, waits for them, and re-layouts: 4.47 us -> none
where the time goes in v11:
time: 111 us
  Pallas kernels  108 us (97%)
  local copies, waits for them, and re-layouts  2.8 us (3%)
    pallas_call x1, Pallas kernels, fused(): pl.pallas_call(functools.partial(fused_kernel, n_pair, n_mo, N_CHUNK), ou...  103 us
    pallas_call x1, Pallas kernels, combine(): pl.pallas_call(combine_kernel, out_shape=jax.ShapeDtypeStruct(pieces.shap...  5.7 us
    reshape x2, local copies, waits for them, and re-layouts, on_device(): ct = coeffs.reshape(n_mo, r_loc, nmo).transpose(0, 2, 1)  2.8 us

profile of v11, /device:TPU:1, one launch (start us, length us, event | category | flops | bytes accessed | tf_op | source)
XLA Modules:
  0.0 111.1 jit_solution(12441965537672463576)
XLA Ops:
  0.0 1.5 %reshape.6 = bf16[4,250,512]{2,1,0:T(8,128)(2,1)S(1)} reshape(bf16[1000,512]{1,0:T(8,128)(2,1)} %c_ref.1) | data formatting | bytes 2048000 | tf_op jit(solution)/shard_map/reshape | solution.py:160
  1.5 1.3 %copy.4 = bf16[4,250,512]{1,2,0:T(8,128)(2,1)} copy(bf16[4,250,512]{2,1,0:T(8,128)(2,1)S(1)} %reshape.6) | data formatting | bytes 2048000 | tf_op jit(solution)/shard_map/reshape | solution.py:160
  2.8 102.6 %shard_map.37 = bf16[64,16,8,128]{3,2,1,0:T(8,128)(2,1)} custom-call(bf16[250,16,1000]{2,1,0:T(8,128)(2,1)} %bitcast.4, bf16[1000,512]{1,0:T(8,128)(2,1)} %c_ref.1, bf16[4,512,250]{2,1,0:T(8,128)(2,1)} %bitcast.5), custom_call_target="tpu_custom_call" | custom-call | tf_op jit(solution)/shard_map/pallas_call | solution.py:113
  105.4 5.7 %shard_map.38 = f32[1024,8,128]{2,1,0:T(8,128)} custom-call(s32[1024]{0:T(1024)} %mirror_ref.1, bf16[1024,8,128]{2,1,0:T(8,128)(2,1)} %bitcast.3), custom_call_target="tpu_custom_call" | custom-call | tf_op jit(solution)/shard_map/pallas_call | solution.py:145

commit v12 on v11

--- a/solution.py
+++ b/solution.py
@@ -58,7 +58,6 @@
     lax.fori_loop(1, n_pair, greet, 0)
     for s in range(1, n_mo):
         pl.semaphore_signal(barrier, 1, device_id=(me, lax.rem(mo + s, n_mo)), device_id_type=MESH)
-    pl.semaphore_wait(barrier, n_pair - 1 + n_mo - 1)
 
     jw = q_ref.shape[-1]
     for c in range(n_chunk):
@@ -70,6 +69,8 @@
             for b in range(n_mo):
                 q_ref[b, k] = res[:, b * jw:(b + 1) * jw]
         own_mo(c).start()
+        if c == 0:
+            pl.semaphore_wait(barrier, n_pair - 1 + n_mo - 1)
         for s in range(1, n_mo):
             mo_copy(c, s).start()
 

time: 111 us -> 108 us (0.973)
  Pallas kernels: 108 us -> 105 us
    pallas_call x1, Pallas kernels: 103 us -> 99.5 us  [fused(): pl.pallas_call(functools.partial(fused_kernel, n_pair, n_mo, N_CHUNK), ou...]
where the time goes in v12:
time: 108 us
  Pallas kernels  105 us (97%)
  local copies, waits for them, and re-layouts  2.8 us (3%)
    pallas_call x1, Pallas kernels, fused(): pl.pallas_call(functools.partial(fused_kernel, n_pair, n_mo, N_CHUNK), ou...  99.5 us
    pallas_call x1, Pallas kernels, combine(): pl.pallas_call(combine_kernel, out_shape=jax.ShapeDtypeStruct(pieces.shap...  5.7 us
    reshape x2, local copies, waits for them, and re-layouts, on_device(): ct = coeffs.reshape(n_mo, r_loc, nmo).transpose(0, 2, 1)  2.8 us

profile of v12, /device:TPU:1, one launch (start us, length us, event | category | flops | bytes accessed | tf_op | source)
XLA Modules:
  0.0 108.0 jit_solution(11413989068853582887)
XLA Ops:
  0.0 1.5 %reshape.6 = bf16[4,250,512]{2,1,0:T(8,128)(2,1)S(1)} reshape(bf16[1000,512]{1,0:T(8,128)(2,1)} %c_ref.1) | data formatting | bytes 2048000 | tf_op jit(solution)/shard_map/reshape | solution.py:161
  1.5 1.3 %copy.4 = bf16[4,250,512]{1,2,0:T(8,128)(2,1)} copy(bf16[4,250,512]{2,1,0:T(8,128)(2,1)S(1)} %reshape.6) | data formatting | bytes 2048000 | tf_op jit(solution)/shard_map/reshape | solution.py:161
  2.8 99.5 %shard_map.37 = bf16[64,16,8,128]{3,2,1,0:T(8,128)(2,1)} custom-call(bf16[250,16,1000]{2,1,0:T(8,128)(2,1)} %bitcast.4, bf16[1000,512]{1,0:T(8,128)(2,1)} %c_ref.1, bf16[4,512,250]{2,1,0:T(8,128)(2,1)} %bitcast.5), custom_call_target="tpu_custom_call" | custom-call | tf_op jit(solution)/shard_map/pallas_call | solution.py:114
  102.3 5.7 %shard_map.38 = f32[1024,8,128]{2,1,0:T(8,128)} custom-call(s32[1024]{0:T(1024)} %mirror_ref.1, bf16[1024,8,128]{2,1,0:T(8,128)(2,1)} %bitcast.3), custom_call_target="tpu_custom_call" | custom-call | tf_op jit(solution)/shard_map/pallas_call | solution.py:146

commit v13 on v12

--- a/solution.py
+++ b/solution.py
@@ -8,7 +8,7 @@
 from jax.sharding import PartitionSpec as P
 
 MESH = pl.DeviceIdType.MESH
-N_CHUNK = 4
+N_CHUNK = 8
 
 
 def fused_kernel(n_pair, n_mo, n_chunk, x_ref, c_ref, ct_ref, held,

time: 108 us -> 109 us (level)
    pallas_call x1, Pallas kernels: 99.5 us -> 101 us  [fused(): pl.pallas_call(functools.partial(fused_kernel, n_pair, n_mo, N_CHUNK), ou...]
where the time goes in v13:
time: 109 us
  Pallas kernels  106 us (97%)
  local copies, waits for them, and re-layouts  2.8 us (3%)
    pallas_call x1, Pallas kernels, fused(): pl.pallas_call(functools.partial(fused_kernel, n_pair, n_mo, N_CHUNK), ou...  101 us
    pallas_call x1, Pallas kernels, combine(): pl.pallas_call(combine_kernel, out_shape=jax.ShapeDtypeStruct(pieces.shap...  5.7 us
    reshape x2, local copies, waits for them, and re-layouts, on_device(): ct = coeffs.reshape(n_mo, r_loc, nmo).transpose(0, 2, 1)  2.8 us

profile of v13, /device:TPU:1, one launch (start us, length us, event | category | flops | bytes accessed | tf_op | source)
XLA Modules:
  0.0 109.2 jit_solution(1637019593029819389)
XLA Ops:
  0.0 1.5 %reshape.6 = bf16[4,250,512]{2,1,0:T(8,128)(2,1)S(1)} reshape(bf16[1000,512]{1,0:T(8,128)(2,1)} %c_ref.1) | data formatting | bytes 2048000 | tf_op jit(solution)/shard_map/reshape | solution.py:161
  1.5 1.3 %copy.4 = bf16[4,250,512]{1,2,0:T(8,128)(2,1)} copy(bf16[4,250,512]{2,1,0:T(8,128)(2,1)S(1)} %reshape.6) | data formatting | bytes 2048000 | tf_op jit(solution)/shard_map/reshape | solution.py:161
  2.8 100.7 %shard_map.37 = bf16[64,16,8,128]{3,2,1,0:T(8,128)(2,1)} custom-call(bf16[250,16,1000]{2,1,0:T(8,128)(2,1)} %bitcast.4, bf16[1000,512]{1,0:T(8,128)(2,1)} %c_ref.1, bf16[4,512,250]{2,1,0:T(8,128)(2,1)} %bitcast.5), custom_call_target="tpu_custom_call" | custom-call | tf_op jit(solution)/shard_map/pallas_call | solution.py:114
  103.5 5.7 %shard_map.38 = f32[1024,8,128]{2,1,0:T(8,128)} custom-call(s32[1024]{0:T(1024)} %mirror_ref.1, bf16[1024,8,128]{2,1,0:T(8,128)(2,1)} %bitcast.3), custom_call_target="tpu_custom_call" | custom-call | tf_op jit(solution)/shard_map/pallas_call | solution.py:146

commit v14 on v12

--- a/solution.py
+++ b/solution.py
@@ -81,9 +81,11 @@
 
         def transform(t, carry):
             k = c * kc + t
-            acc = jnp.dot(ct_ref[0], arrived[0, k], preferred_element_type=jnp.float32)
+            r_loc = arrived.shape[2]
+            acc = jnp.dot(ct_ref[:, 0:r_loc], arrived[0, k], preferred_element_type=jnp.float32)
             for b in range(1, n_mo):
-                acc += jnp.dot(ct_ref[b], arrived[b, k], preferred_element_type=jnp.float32)
+                cols = ct_ref[:, b * r_loc:(b + 1) * r_loc]
+                acc += jnp.dot(cols, arrived[b, k], preferred_element_type=jnp.float32)
             sendbuf[k] = acc.reshape(n_pair, -1, acc.shape[-1]).astype(sendbuf.dtype)
             return carry
 
@@ -158,7 +160,7 @@
     def on_device(integrals, coeffs, mirror):
         rows, r_loc, nbf = integrals.shape
         nmo = coeffs.shape[1]
-        ct = coeffs.reshape(n_mo, r_loc, nmo).transpose(0, 2, 1)
+        ct = coeffs.T
         held = fused(integrals, coeffs, ct, n_pair, n_mo)
         return combine(held.reshape(-1, *held.shape[2:]), mirror)
 

time: 108 us -> 109 us (level)
  Pallas kernels: 105 us -> 107 us
    reshape x2 -> x0, local copies, waits for them, and re-layouts: 2.8 us -> none  [on_device(): ct = coeffs.reshape(n_mo, r_loc, nmo).transpose(0, 2, 1)]
    unnamed x0 -> x1, local copies, waits for them, and re-layouts: none -> 2.26 us
    pallas_call x1, Pallas kernels: 99.5 us -> 101 us  [fused(): pl.pallas_call(functools.partial(fused_kernel, n_pair, n_mo, N_CHUNK), ou...]
where the time goes in v14:
time: 109 us
  Pallas kernels  107 us (98%)
  local copies, waits for them, and re-layouts  2.26 us (2%)
    pallas_call x1, Pallas kernels, fused(): pl.pallas_call(functools.partial(fused_kernel, n_pair, n_mo, N_CHUNK), ou...  101 us
    pallas_call x1, Pallas kernels, combine(): pl.pallas_call(combine_kernel, out_shape=jax.ShapeDtypeStruct(pieces.shap...  5.7 us
    unnamed x1, local copies, waits for them, and re-layouts  2.26 us

profile of v14, /device:TPU:1, one launch (start us, length us, event | category | flops | bytes accessed | tf_op | source)
XLA Modules:
  0.0 108.9 jit_solution(3953672003636273880)
XLA Ops:
  0.0 2.3 %copy.4 = bf16[1000,512]{0,1:T(8,128)(2,1)} copy(bf16[1000,512]{1,0:T(8,128)(2,1)} %c_ref.1) | data formatting | bytes 2048000 | tf_op args[1]
  2.3 100.9 %shard_map.37 = bf16[64,16,8,128]{3,2,1,0:T(8,128)(2,1)} custom-call(bf16[250,16,1000]{2,1,0:T(8,128)(2,1)} %bitcast.4, bf16[1000,512]{1,0:T(8,128)(2,1)} %c_ref.1, bf16[512,1000]{1,0:T(8,128)(2,1)} %bitcast.5), custom_call_target="tpu_custom_call" | custom-call | tf_op jit(solution)/shard_map/pallas_call | solution.py:116
  103.2 5.7 %shard_map.38 = f32[1024,8,128]{2,1,0:T(8,128)} custom-call(s32[1024]{0:T(1024)} %mirror_ref.1, bf16[1024,8,128]{2,1,0:T(8,128)(2,1)} %bitcast.3), custom_call_target="tpu_custom_call" | custom-call | tf_op jit(solution)/shard_map/pallas_call | solution.py:148

commit v15 on v12

--- a/solution.py
+++ b/solution.py
@@ -133,13 +133,16 @@
 
 
 def combine_kernel(mirror_ref, x_ref, o_ref):
-    def body(k, carry):
-        a = x_ref[k].astype(jnp.float32)
-        b = x_ref[mirror_ref[k]].astype(jnp.float32)
-        o_ref[k] = 0.5 * (a + b)
+    step = 16
+
+    def body(g, carry):
+        k0 = pl.multiple_of(g * step, step)
+        a = x_ref[pl.ds(k0, step)].astype(jnp.float32)
+        b = jnp.stack([x_ref[mirror_ref[k0 + t]] for t in range(step)])
+        o_ref[pl.ds(k0, step)] = 0.5 * (a + b.astype(jnp.float32))
         return carry
 
-    lax.fori_loop(0, x_ref.shape[0], body, 0, unroll=8)
+    lax.fori_loop(0, x_ref.shape[0] // step, body, 0)
 
 
 def combine(pieces, mirror):

time: 108 us -> 108 us (level)
  no operation moved by 1% of the time
where the time goes in v15:
time: 108 us
  Pallas kernels  105 us (97%)
  local copies, waits for them, and re-layouts  2.8 us (3%)
    pallas_call x1, Pallas kernels, fused(): pl.pallas_call(functools.partial(fused_kernel, n_pair, n_mo, N_CHUNK), ou...  99.5 us
    pallas_call x1, Pallas kernels, combine(): pl.pallas_call(combine_kernel, out_shape=jax.ShapeDtypeStruct(pieces.shap...  5.23 us
    reshape x2, local copies, waits for them, and re-layouts, on_device(): ct = coeffs.reshape(n_mo, r_loc, nmo).transpose(0, 2, 1)  2.8 us

profile of v15, /device:TPU:1, one launch (start us, length us, event | category | flops | bytes accessed | tf_op | source)
XLA Modules:
  0.0 107.5 jit_solution(15948414504002365505)
XLA Ops:
  0.0 1.5 %reshape.6 = bf16[4,250,512]{2,1,0:T(8,128)(2,1)S(1)} reshape(bf16[1000,512]{1,0:T(8,128)(2,1)} %c_ref.1) | data formatting | bytes 2048000 | tf_op jit(solution)/shard_map/reshape | solution.py:164
  1.5 1.3 %copy.4 = bf16[4,250,512]{1,2,0:T(8,128)(2,1)} copy(bf16[4,250,512]{2,1,0:T(8,128)(2,1)S(1)} %reshape.6) | data formatting | bytes 2048000 | tf_op jit(solution)/shard_map/reshape | solution.py:164
  2.8 99.5 %shard_map.37 = bf16[64,16,8,128]{3,2,1,0:T(8,128)(2,1)} custom-call(bf16[250,16,1000]{2,1,0:T(8,128)(2,1)} %bitcast.4, bf16[1000,512]{1,0:T(8,128)(2,1)} %c_ref.1, bf16[4,512,250]{2,1,0:T(8,128)(2,1)} %bitcast.5), custom_call_target="tpu_custom_call" | custom-call | tf_op jit(solution)/shard_map/pallas_call | solution.py:114
  102.3 5.2 %shard_map.38 = f32[1024,8,128]{2,1,0:T(8,128)} custom-call(s32[1024]{0:T(1024)} %mirror_ref.1, bf16[1024,8,128]{2,1,0:T(8,128)(2,1)} %bitcast.3), custom_call_target="tpu_custom_call" | custom-call | tf_op jit(solution)/shard_map/pallas_call | solution.py:149

commit v16 on v15

--- a/solution.py
+++ b/solution.py
@@ -8,7 +8,7 @@
 from jax.sharding import PartitionSpec as P
 
 MESH = pl.DeviceIdType.MESH
-N_CHUNK = 4
+N_CHUNK = 2
 
 
 def fused_kernel(n_pair, n_mo, n_chunk, x_ref, c_ref, ct_ref, held,

time: 108 us -> 116 us (1.074)
  the two profiles are of different devices: /device:TPU:1 before, /device:TPU:7 now
where the time goes in v16:
time: 116 us
  Pallas kernels  113 us (97%)
  local copies, waits for them, and re-layouts  2.8 us (2%)
    pallas_call x1, Pallas kernels, fused(): pl.pallas_call(functools.partial(fused_kernel, n_pair, n_mo, N_CHUNK), ou...  108 us
    pallas_call x1, Pallas kernels, combine(): pl.pallas_call(combine_kernel, out_shape=jax.ShapeDtypeStruct(pieces.shap...  5.23 us
    reshape x2, local copies, waits for them, and re-layouts, on_device(): ct = coeffs.reshape(n_mo, r_loc, nmo).transpose(0, 2, 1)  2.8 us

profile of v16, /device:TPU:7, one launch (start us, length us, event | category | flops | bytes accessed | tf_op | source)
XLA Modules:
  0.0 115.8 jit_solution(13304724897886969068)
XLA Ops:
  0.0 1.5 %reshape.6 = bf16[4,250,512]{2,1,0:T(8,128)(2,1)S(1)} reshape(bf16[1000,512]{1,0:T(8,128)(2,1)} %c_ref.1) | data formatting | bytes 2048000 | tf_op jit(solution)/shard_map/reshape | solution.py:164
  1.5 1.3 %copy.4 = bf16[4,250,512]{1,2,0:T(8,128)(2,1)} copy(bf16[4,250,512]{2,1,0:T(8,128)(2,1)S(1)} %reshape.6) | data formatting | bytes 2048000 | tf_op jit(solution)/shard_map/reshape | solution.py:164
  2.8 107.7 %shard_map.37 = bf16[64,16,8,128]{3,2,1,0:T(8,128)(2,1)} custom-call(bf16[250,16,1000]{2,1,0:T(8,128)(2,1)} %bitcast.4, bf16[1000,512]{1,0:T(8,128)(2,1)} %c_ref.1, bf16[4,512,250]{2,1,0:T(8,128)(2,1)} %bitcast.5), custom_call_target="tpu_custom_call" | custom-call | tf_op jit(solution)/shard_map/pallas_call | solution.py:114
  110.5 5.2 %shard_map.38 = f32[1024,8,128]{2,1,0:T(8,128)} custom-call(s32[1024]{0:T(1024)} %mirror_ref.1, bf16[1024,8,128]{2,1,0:T(8,128)(2,1)} %bitcast.3), custom_call_target="tpu_custom_call" | custom-call | tf_op jit(solution)/shard_map/pallas_call | solution.py:149

commit v17 on v15

--- a/solution.py
+++ b/solution.py
@@ -133,7 +133,7 @@
 
 
 def combine_kernel(mirror_ref, x_ref, o_ref):
-    step = 16
+    step = 32
 
     def body(g, carry):
         k0 = pl.multiple_of(g * step, step)

time: 108 us -> 107 us (level)
  no operation moved by 1% of the time
where the time goes in v17:
time: 107 us
  Pallas kernels  104 us (97%)
  local copies, waits for them, and re-layouts  2.8 us (3%)
    pallas_call x1, Pallas kernels, fused(): pl.pallas_call(functools.partial(fused_kernel, n_pair, n_mo, N_CHUNK), ou...  99.5 us
    pallas_call x1, Pallas kernels, combine(): pl.pallas_call(combine_kernel, out_shape=jax.ShapeDtypeStruct(pieces.shap...  4.95 us
    reshape x2, local copies, waits for them, and re-layouts, on_device(): ct = coeffs.reshape(n_mo, r_loc, nmo).transpose(0, 2, 1)  2.8 us

profile of v17, /device:TPU:1, one launch (start us, length us, event | category | flops | bytes accessed | tf_op | source)
XLA Modules:
  0.0 107.3 jit_solution(6315932163551970994)
XLA Ops:
  0.0 1.5 %reshape.6 = bf16[4,250,512]{2,1,0:T(8,128)(2,1)S(1)} reshape(bf16[1000,512]{1,0:T(8,128)(2,1)} %c_ref.1) | data formatting | bytes 2048000 | tf_op jit(solution)/shard_map/reshape | solution.py:164
  1.5 1.3 %copy.4 = bf16[4,250,512]{1,2,0:T(8,128)(2,1)} copy(bf16[4,250,512]{2,1,0:T(8,128)(2,1)S(1)} %reshape.6) | data formatting | bytes 2048000 | tf_op jit(solution)/shard_map/reshape | solution.py:164
  2.8 99.5 %shard_map.37 = bf16[64,16,8,128]{3,2,1,0:T(8,128)(2,1)} custom-call(bf16[250,16,1000]{2,1,0:T(8,128)(2,1)} %bitcast.4, bf16[1000,512]{1,0:T(8,128)(2,1)} %c_ref.1, bf16[4,512,250]{2,1,0:T(8,128)(2,1)} %bitcast.5), custom_call_target="tpu_custom_call" | custom-call | tf_op jit(solution)/shard_map/pallas_call | solution.py:114
  102.3 4.9 %shard_map.38 = f32[1024,8,128]{2,1,0:T(8,128)} custom-call(s32[1024]{0:T(1024)} %mirror_ref.1, bf16[1024,8,128]{2,1,0:T(8,128)(2,1)} %bitcast.3), custom_call_target="tpu_custom_call" | custom-call | tf_op jit(solution)/shard_map/pallas_call | solution.py:149
